TPU v7x, 128 devices: a whole 4x4x4 slice. The times are simulated.
128 devices in a mesh: kv: 4 (over y), seq: 32 (over z, x, core).
Axes of the slice: x: 4, y: 4, z: 4, core: 2. Of those that a mesh axis runs over, the one named last changes fastest.
Arguments:
- queries: bfloat16 [32768, 4096], P('seq', 'kv'), may hold values from -40 to 40
- query_tangent: bfloat16 [32768, 4096], P('seq', 'kv'), may hold values from -6 to 6
- key_value: bfloat16 [32768, 2, 512], P('seq', None, 'kv'), may hold values from -40 to 40
- key_value_tangents: bfloat16 [32768, 2, 512], P('seq', None, 'kv'), may hold values from -6 to 6
- doc_lengths: int32 [256], replicated, may hold values from 1 to 1024, 32768 in all
- out_weight: bfloat16 [4096, 2048], P(('kv', 'seq')), may hold values from -1 to 1
- weight_tangent: bfloat16 [4096, 2048], P(('kv', 'seq')), may hold values from -0.25 to 0.25
Outputs:
- layer_out: bfloat16 [32768, 2048], P('seq', 'kv')
- out_tangent: bfloat16 [32768, 2048], P('seq', 'kv')
Inputs may be any that keep to these rules, and one draw needn't show every extreme that they name: `doc_lengths`: the 256 lengths sum to 32768; the longest is exactly 1024.
All inputs are finite; a program needn't handle non-finite values.
Results may differ from a plain program's by a relative error of at most 0.0057.
Values may be sent and summed in bfloat16 or wider, within the bound.
A program may use at most 128 MiB of HBM per device.

v0:
```python
import math

import jax
import jax.numpy as jnp
from jax import lax
from jax.sharding import PartitionSpec as P

STRETCH = 32
WINDOW = 224


masked_score = -1e30


def passed_along(block, axis, distance):
    devices = range(lax.axis_size(axis))
    route = [(i - distance, i) for i in devices if i - distance in devices]
    return lax.ppermute(block, axis, route)


def attend(query_block, query_tan, key_rows, value_rows, key_tangent, value_tangent, lower_rel):
    head_dim = key_rows.shape[-1]
    score_scale = 1.0 / math.sqrt(head_dim)
    scores = (
        jnp.einsum("bcgh,brh->bgcr", query_block, key_rows, preferred_element_type=jnp.float32)
        * score_scale
    )
    tangent = (
        jnp.einsum("bcgh,brh->bgcr", query_tan, key_rows, preferred_element_type=jnp.float32)
        + jnp.einsum("bcgh,brh->bgcr", query_block, key_tangent, preferred_element_type=jnp.float32)
    ) * score_scale
    columns = jnp.arange(key_rows.shape[1]).astype(jnp.float32)[None, None, None, :]
    row_index = jnp.arange(query_block.shape[1]).astype(jnp.float32)[None, None, :, None]
    admitted = (columns >= lower_rel.astype(jnp.float32)[:, None, :, None]) & (
        columns <= row_index + WINDOW
    )
    scores = jnp.where(admitted, scores, masked_score)
    row_peak = jnp.max(scores, axis=-1, keepdims=True)
    exponent = jnp.where(admitted, jnp.exp(scores - row_peak), 0.0)
    row_total = jnp.sum(exponent, axis=-1, keepdims=True)
    probabilities = exponent / row_total
    tangent = jnp.where(admitted, tangent, 0.0)
    mean_tan = jnp.sum(probabilities * tangent, axis=-1, keepdims=True)
    prob_low = probabilities.astype(jnp.bfloat16)
    tangent_low = (probabilities * (tangent - mean_tan)).astype(jnp.bfloat16)
    outputs = jnp.einsum("bgcr,brh->bcgh", prob_low, value_rows, preferred_element_type=jnp.float32)
    out_tan = jnp.einsum(
        "bgcr,brh->bcgh", tangent_low, value_rows, preferred_element_type=jnp.float32
    ) + jnp.einsum("bgcr,brh->bcgh", prob_low, value_tangent, preferred_element_type=jnp.float32)
    return (outputs.astype(jnp.bfloat16), out_tan.astype(jnp.bfloat16))


def body(
    queries, query_tangent, key_value, key_value_tangents, doc_lengths, out_weight, weight_tangent
):
    local_tokens = queries.shape[0]
    head_dim = key_value.shape[2]
    group_width = queries.shape[1]
    heads_per_group = group_width // head_dim
    seq_index = lax.axis_index("seq")
    stretch_count = local_tokens // STRETCH
    span_count = (WINDOW + STRETCH) // STRETCH
    lead_blocks = WINDOW // STRETCH
    stacked = jnp.concatenate(
        [
            key_value.reshape(local_tokens, 2 * head_dim),
            key_value_tangents.reshape(local_tokens, 2 * head_dim),
        ],
        axis=1,
    )
    prior = passed_along(stacked[local_tokens - WINDOW :], "seq", 1)
    context = jnp.concatenate([prior, stacked], axis=0).reshape(
        lead_blocks + stretch_count, STRETCH, 4 * head_dim
    )
    windows = jnp.concatenate(
        [context[offset : offset + stretch_count] for offset in range(span_count)], axis=1
    )
    doc_ends = jnp.cumsum(doc_lengths)
    doc_starts = doc_ends - doc_lengths
    position = seq_index * local_tokens + jnp.arange(local_tokens, dtype=jnp.int32)
    inside = (doc_starts[None, :] <= position[:, None]) & (position[:, None] < doc_ends[None, :])
    doc_first = jnp.sum(jnp.where(inside, doc_starts[None, :], 0), axis=1)
    lower_bound = jnp.maximum(doc_first, position - WINDOW + 1)
    stretch_start = position.reshape(stretch_count, STRETCH)[:, :1]
    lower_rel = lower_bound.reshape(stretch_count, STRETCH) - (stretch_start - WINDOW)
    packed = jnp.concatenate([queries, query_tangent], axis=1).reshape(
        stretch_count, STRETCH, 2 * group_width
    )
    lead_shape = packed.shape[:-2]
    query_block = packed[..., :group_width].reshape(-1, STRETCH, heads_per_group, head_dim)
    query_tan = packed[..., group_width:].reshape(-1, STRETCH, heads_per_group, head_dim)
    outputs, out_tan = attend(
        query_block,
        query_tan,
        windows[..., :head_dim],
        windows[..., head_dim : 2 * head_dim],
        windows[..., 2 * head_dim : 3 * head_dim],
        windows[..., 3 * head_dim :],
        lower_rel,
    )
    attention_home = outputs.reshape(lead_shape + (STRETCH, group_width))
    tangent_home = out_tan.reshape(lead_shape + (STRETCH, group_width))
    attention = attention_home.reshape(local_tokens, group_width)
    attention_tan = tangent_home.reshape(local_tokens, group_width)
    full_weight, full_tangent = (
        lax.all_gather(out_weight, "seq", axis=0, tiled=True),
        lax.all_gather(weight_tangent, "seq", axis=0, tiled=True),
    )
    partial_value = jnp.dot(attention, full_weight, preferred_element_type=jnp.float32)
    partial_tan = jnp.dot(attention_tan, full_weight, preferred_element_type=jnp.float32) + jnp.dot(
        attention, full_tangent, preferred_element_type=jnp.float32
    )
    layer_out, out_tangent = (
        lax.psum_scatter(partial_value, "kv", scatter_dimension=1, tiled=True),
        lax.psum_scatter(partial_tan, "kv", scatter_dimension=1, tiled=True),
    )
    return (layer_out.astype(jnp.bfloat16), out_tangent.astype(jnp.bfloat16))


def solution(mesh):
    in_specs = (
        P("seq", "kv"),
        P("seq", "kv"),
        P("seq", None, "kv"),
        P("seq", None, "kv"),
        P(),
        P(("kv", "seq"), None),
        P(("kv", "seq"), None),
    )
    out_specs = (P("seq", "kv"), P("seq", "kv"))
    return jax.shard_map(body, mesh=mesh, in_specs=in_specs, out_specs=out_specs, check_vma=False)
```

profile of v0, /device:TPU:0, one launch (start us, length us, event | category | flops | bytes accessed | tf_op | source)
XLA Modules:
  0.0 288.7 jit_solution(2605491856602272903)
XLA Ops:
  7.2 0.7 all-gather.3.cloned.1.call-update
  8.0 1.1 bitcast_dynamic-update-slice_fusion.1
  9.1 1.1 bitcast_dynamic-update-slice_fusion
  10.2 2.0 collective-permute-start
  12.3 2.2 concatenate.21
  14.4 1.1 concatenate.22
  15.6 2.7 pad_maximum_fusion
  18.3 2.4 slice_bitcast_fusion.4
  20.7 0.3 reduce-window.9
  21.3 0.4 select_reduce_fusion
  22.3 2.2 pad_maximum_fusion.1
  25.3 0.6 copy-done.4
  26.1 4.5 %fusion.17 = f32[32,256,32,8]{1,2,3,0:T(8,128)} fusion(bf16[32,4,8,8,128]{4,3,2,1,0:T(8,128)(2,1)S(1)} %get-tuple-element.5, bf16[32,256,512]{2,1,0:T(8,128)(2,1)S(1)} %maximum_dynamic-update-slice_fusion), kind=kOutput, calls=%fused_computation.32 | convolution fusion | flops 536870912 | bytes 12582912 | tf_op jit(solution)/shard_map/bcgh,brh->bgcr/dot_general | solution.py:25
  30.6 1.6 copy-done.1
  32.2 1.3 fusion.13
  33.5 12.9 %fusion.41 = (f32[32,8,32]{2,1,0:T(8,128)S(1)}, f32[32,8,32,256]{3,2,1,0:T(8,128)}) fusion(f32[32,256,32,8]{1,2,3,0:T(8,128)} %fusion.17, pred[32,32,256]{2,1,0:T(8,128)(4,1)S(1)} %compare_and_fusion), kind=kOutput, calls=%fused_computation.87 | output fusion | flops 14680319 | bytes 17072128 | tf_op jit(solution)/shard_map/sub | solution.py:39
  46.3 7.9 %multiply_reduce_fusion = (f32[32,8,32]{2,1,0:T(8,128)S(1)}, f32[32,8,32,256]{3,2,1,0:T(8,128)}) fusion(f32[32,8,32,256]{3,2,1,0:T(8,128)} %get-tuple-element.14, f32[32,8,32]{2,1,0:T(8,128)S(1)} %get-tuple-element.13, f32[32,256,32,8]{1,2,3,0:T(8,128)S(1)} %fusion.13, bf16[32,4,8,8,128]{4,3,2,1,0:T(8,128)(2,1)S(1)} %get-tuple-element.5, ...), kind=kOutput, calls=%fused_computation.4 | convolution fusion | flops 549445632 | bytes 29687808 | tf_op jit(solution)/shard_map/bcgh,brh->bgcr/dot_general | solution.py:30
  54.3 9.7 %fusion.2 = f32[32,128,8,32]{1,3,2,0:T(8,128)} fusion(f32[32,8,32,256]{3,2,1,0:T(8,128)} %get-tuple-element.16, f32[32,8,32]{2,1,0:T(8,128)S(1)} %get-tuple-element.15, bf16[32,256,512]{2,1,0:T(8,128)(2,1)} %copy-done.1, f32[32,8,32,256]{3,2,1,0:T(8,128)} %get-tuple-element.14, f32[32,8,32]{2,1,0:T(8,128)S(1)} %get-tuple-element.13), kind=kOutput, calls=%fused_computation.7 | convolution fusion | flops 545259520 | bytes 23134208 | tf_op jit(solution)/shard_map/bgcr,brh->bcgh/dot_general | solution.py:47
  64.0 0.9 copy-done.2
  64.9 2.4 copy-done.7
  67.3 4.3 %fusion.28 = bf16[32,32,8,128]{3,1,2,0:T(8,128)(2,1)S(1)} fusion(f32[32,128,8,32]{1,3,2,0:T(8,128)} %fusion.2, bf16[32,256,512]{2,1,0:T(8,128)(2,1)S(1)} %copy-done.2, f32[32,8,32,256]{3,2,1,0:T(8,128)S(1)} %copy-done.7, f32[32,8,32]{2,1,0:T(8,128)S(1)} %get-tuple-element.13), kind=kOutput, calls=%fused_computation.48 | convolution fusion | flops 543162368 | bytes 16908288 | tf_op jit(solution)/shard_map/bgcr,brh->bcgh/dot_general | solution.py:49
  71.6 2.3 copy.24
  73.9 4.3 %convert_bitcast_fusion = bf16[32,32,8,128]{3,1,2,0:T(8,128)(2,1)S(1)} fusion(bf16[32,256,512]{2,1,0:T(8,128)(2,1)S(1)} %copy-done.2, f32[32,8,32,256]{3,2,1,0:T(8,128)} %get-tuple-element.14, f32[32,8,32]{2,1,0:T(8,128)S(1)} %get-tuple-element.13), kind=kOutput, calls=%fused_computation.40 | convolution fusion | flops 542113792 | bytes 12713984 | tf_op jit(solution)/shard_map/bgcr,brh->bcgh/dot_general | solution.py:46
  78.3 1.0 copy.21
  79.3 10.6 %fusion.7 = f32[1024,2048]{1,0:T(8,128)} fusion(bf16[1024,2048]{1,0:T(8,128)(2,1)} %all-gather.3.cloned.1.call-done, bf16[128,8,8,128]{3,2,1,0:T(8,128)(2,1)} %bitcast.100), kind=kOutput, calls=%fused_computation.22 | convolution fusion | flops 4294967296 | bytes 14680064 | tf_op jit(solution)/shard_map/dot_general | solution.py:110
  89.9 16.8 %all-gather.5.cloned.1.call-done = bf16[1024,2048]{1,0:T(8,128)(2,1)} async-done(((bf16[32,2048]{1,0:T(8,128)(2,1)}), bf16[1024,2048]{1,0:T(8,128)(2,1)}) %all-gather.5.cloned.1.call-update) | async-done | bytes 4194320 | tf_op jit(solution)/shard_map/all_gather | solution.py:107
  106.7 10.1 %convolution_add_fusion = f32[1024,2048]{1,0:T(8,128)} fusion(f32[1024,2048]{1,0:T(8,128)} %fusion.7, bf16[1024,2048]{1,0:T(8,128)(2,1)} %all-gather.5.cloned.1.call-done, bf16[128,8,8,128]{3,2,1,0:T(8,128)(2,1)S(1)} %bitcast.98), kind=kOutput, calls=%fused_computation.15 | convolution fusion | flops 4297064448 | bytes 23068672 | tf_op jit(solution)/shard_map/dot_general | solution.py:110
  116.9 9.1 %fusion.11 = f32[1024,2048]{1,0:T(8,128)} fusion(bf16[1024,2048]{1,0:T(8,128)(2,1)} %all-gather.3.cloned.1.call-done, bf16[128,8,8,128]{3,2,1,0:T(8,128)(2,1)S(1)} %bitcast.99), kind=kOutput, calls=%fused_computation.26 | convolution fusion | flops 4294967296 | bytes 14680064 | tf_op jit(solution)/shard_map/dot_general | solution.py:109
  126.0 70.8 %reduce-scatter.5.cloned.1.call-done = f32[1024,512]{1,0:T(8,128)} async-done(((f32[1024,2048]{1,0:T(8,128)}), f32[1024,512]{1,0:T(8,128)}) %reduce-scatter.5.cloned.1.call-update) | async-done | bytes 2097168 | tf_op jit(solution)/shard_map/reduce_scatter | solution.py:115
  196.9 2.7 convert_element_type.56
  199.5 79.9 %reduce-scatter.3.cloned.1.call-done = f32[1024,512]{1,0:T(8,128)} async-done(((f32[1024,2048]{1,0:T(8,128)}), f32[1024,512]{1,0:T(8,128)}) %reduce-scatter.3.cloned.1.call-update) | async-done | bytes 2097168 | tf_op jit(solution)/shard_map/reduce_scatter | solution.py:114
  279.5 2.7 convert_element_type.52
  (43 shorter events, 2.2 us)
Async XLA Ops:
  7.2 7.3 %copy-start.3 = (bf16[1024,2,128]{2,1,0:T(2,128)(2,1)S(1)}, bf16[1024,2,128]{2,1,0:T(2,128)(2,1)}, u32[]{:S(2)}) copy-start(bf16[1024,2,128]{2,1,0:T(2,128)(2,1)} %param.10) | copy-start | bytes 1572868
  7.2 72.1 %all-gather.3.cloned.1.call-start = ((), (), s32[]{:S(2)}) async-start(), calls=%async_computation.2 | async-start | bytes 4325376 | tf_op jit(solution)/shard_map/all_gather | solution.py:106
  7.9 98.8 %all-gather.5.cloned.1.call-start = ((), (), s32[]{:S(2)}) async-start(), calls=%async_computation.4 | async-start | bytes 4325376 | tf_op jit(solution)/shard_map/all_gather | solution.py:107
  10.2 12.1 %collective-permute-start = (bf16[224,512]{1,0:T(8,128)(2,1)S(1)}, bf16[224,512]{1,0:T(8,128)(2,1)}, u32[]{:S(2)}, u32[]{:S(2)}) collective-permute-start(bf16[224,512]{1,0:T(8,128)(2,1)S(1)} %slice.99), channel_id=1, source_target_pairs={{0,1},{1,2},{2,3},{3,4},{4,5},{5,6},{6,7},{7,8},{8,9},{9,10},{10,1... | collective-permute-start | bytes 688136 | tf_op jit(solution)/shard_map/ppermute | solution.py:18
  12.2 184.6 %reduce-scatter.5.cloned.1.call-start = ((), (), s32[]{:S(2)}) async-start(), calls=%async_computation.5 | async-start | bytes 10485760 | tf_op jit(solution)/shard_map/reduce_scatter | solution.py:115
  18.3 2.4 copy-start.6
  24.8 1.0 copy-start.4
  24.8 1.2 copy-start.5
  26.1 6.1 %copy-start.1 = (bf16[32,256,512]{2,1,0:T(8,128)(2,1)}, bf16[32,256,512]{2,1,0:T(8,128)(2,1)S(1)}, u32[]{:S(2)}) copy-start(bf16[32,256,512]{2,1,0:T(8,128)(2,1)S(1)} %maximum_dynamic-update-slice_fusion) | copy-start | bytes 25165828
  26.1 6.1 %copy-start = (bf16[32,4,8,8,128]{4,3,2,1,0:T(8,128)(2,1)S(1)}, bf16[32,4,8,8,128]{4,3,2,1,0:T(8,128)(2,1)}, u32[]{:S(2)}) copy-start(bf16[32,4,8,8,128]{4,3,2,1,0:T(8,128)(2,1)} %get-tuple-element.4) | copy-start | bytes 6291460
  54.2 10.6 %copy-start.2 = (bf16[32,256,512]{2,1,0:T(8,128)(2,1)S(1)}, bf16[32,256,512]{2,1,0:T(8,128)(2,1)}, u32[]{:S(2)}) copy-start(bf16[32,256,512]{2,1,0:T(8,128)(2,1)} %copy-done.1) | copy-start | bytes 25165828
  54.2 13.0 %copy-start.7 = (f32[32,8,32,256]{3,2,1,0:T(8,128)S(1)}, f32[32,8,32,256]{3,2,1,0:T(8,128)}, u32[]{:S(2)}) copy-start(f32[32,8,32,256]{3,2,1,0:T(8,128)} %get-tuple-element.14) | copy-start | bytes 25165828
  116.8 162.6 %reduce-scatter.3.cloned.1.call-start = ((), (), s32[]{:S(2)}) async-start(), calls=%async_computation.3 | async-start | bytes 10485760 | tf_op jit(solution)/shard_map/reduce_scatter | solution.py:114
Sparse Core Ops, SparseCore 0:
  10.2 48.6 all-gather.2
  61.2 45.4 all-gather.4
  117.0 79.8 reduce-scatter.4
  199.2 80.2 reduce-scatter.2
where the time goes:
time: 290 us; the launch traced here: 289 us
  waiting for transfers between devices  168 us (58%)
  matrix products  61.8 us (21%)
  other arithmetic  24.6 us (8%)
  local copies, waits for them, and re-layouts  17.8 us (6%)
  between operations  14 us (5%)
    reduce_scatter x1, waiting for transfers between devices, body(): lax.psum_scatter(partial_value, 'kv', scatter_dimension=1, tiled=True)  79.9 us
    reduce_scatter x1, waiting for transfers between devices, body(): lax.psum_scatter(partial_tan, 'kv', scatter_dimension=1, tiled=True)  70.8 us
    all_gather x1, waiting for transfers between devices, body(): lax.all_gather(weight_tangent, 'seq', axis=0, tiled=True)  16.8 us
    sub x1, other arithmetic, attend(): exponent = jnp.where(admitted, jnp.exp(scores - row_peak), 0.0)  12.9 us
    dot_general x1, matrix products, body(): jnp.dot(attention_tan, full_weight, preferred_element_type=jnp.float32)  10.6 us
    dot_general x1, matrix products, body(): jnp.dot(attention, full_tangent, preferred_element_type=jnp.float32)  10.1 us
    unnamed x25, local copies, waits for them, and re-layouts  9.84 us
    dot_general x1, matrix products, attend(): jnp.einsum('bgcr,brh->bcgh', tangent_low, value_rows, preferred_element_t...  9.74 us
  transfers between devices with their start and end apart: 5, of which 3 were waited for; matrix products, arithmetic and copies ran while one was open for 30% of the time, Pallas kernels for 0%

commit v1 on v0

v1 whole, which is shorter than its diff:
```python
import math

import jax
import jax.numpy as jnp
from jax import lax
from jax.experimental import pallas as pl
from jax.experimental.pallas import tpu as pltpu
from jax.sharding import PartitionSpec as P

STRETCH = 32
WINDOW = 224
HEAD = 128
HEADS = 8
SPAN = WINDOW + STRETCH
MASKED = -1e30
SCALE = 1.0 / math.sqrt(HEAD)
EXP_SCALE = SCALE * math.log2(math.e)


def attend_block(q, qt, keys, values, lower_rel):
    rows = STRETCH * HEADS
    qs = jnp.concatenate([q[:, HEAD * h : HEAD * (h + 1)] for h in range(HEADS)], axis=0)
    qts = jnp.concatenate([qt[:, HEAD * h : HEAD * (h + 1)] for h in range(HEADS)], axis=0)
    dims = (((1,), (1,)), ((), ()))
    s = lax.dot_general(qs, keys[:, :HEAD], dims, preferred_element_type=jnp.float32)
    t = lax.dot_general(
        jnp.concatenate([qts, qs], axis=1), keys, dims, preferred_element_type=jnp.float32
    )
    column = lax.broadcasted_iota(jnp.int32, (STRETCH, SPAN), 1)
    row = lax.broadcasted_iota(jnp.int32, (STRETCH, SPAN), 0)
    admitted = (column >= lower_rel) & (column <= row + WINDOW)
    s = jnp.where(admitted[None], s.reshape(HEADS, STRETCH, SPAN), MASKED).reshape(rows, SPAN)
    peak = jnp.max(s, axis=-1, keepdims=True)
    e = jnp.exp2((s - peak) * EXP_SCALE)
    total = jnp.sum(e, axis=-1, keepdims=True)
    inverse = 1.0 / total
    mean = jnp.sum(e * t, axis=-1, keepdims=True) * inverse
    et = e * (t - mean)
    flat = (((1,), (0,)), ((), ()))
    ev = lax.dot_general(e.astype(jnp.bfloat16), values, flat, preferred_element_type=jnp.float32)
    etv = lax.dot_general(
        et.astype(jnp.bfloat16), values[:, :HEAD], flat, preferred_element_type=jnp.float32
    )
    out = (ev[:, :HEAD] * inverse).astype(jnp.bfloat16)
    tan = ((etv * SCALE + ev[:, HEAD:]) * inverse).astype(jnp.bfloat16)
    return out, tan


def attention_kernel(unroll, q_ref, qt_ref, keys_ref, values_ref, lower_ref, out_ref, tan_ref):
    blocks = q_ref.shape[0] // STRETCH

    def step(i, carry):
        at = pl.multiple_of(i * STRETCH, STRETCH)
        here = pl.ds(at, STRETCH)
        span = pl.ds(at, SPAN)
        out, tan = attend_block(
            q_ref[here, :], qt_ref[here, :], keys_ref[span, :], values_ref[span, :],
            lower_ref[here, :1],
        )
        for h in range(HEADS):
            out_ref[here, HEAD * h : HEAD * (h + 1)] = out[STRETCH * h : STRETCH * (h + 1)]
            tan_ref[here, HEAD * h : HEAD * (h + 1)] = tan[STRETCH * h : STRETCH * (h + 1)]
        return carry

    lax.fori_loop(0, blocks, step, 0, unroll=unroll)


def attention(q, qt, keys, values, lower_rel, unroll=2):
    import functools
    vmem = pl.BlockSpec(memory_space=pltpu.VMEM)
    shape = jax.ShapeDtypeStruct(q.shape, jnp.bfloat16)
    return pl.pallas_call(
        functools.partial(attention_kernel, unroll),
        out_shape=(shape, shape),
        in_specs=[vmem] * 5,
        out_specs=(vmem, vmem),
        compiler_params=pltpu.CompilerParams(vmem_limit_bytes=40 << 20),
        name="attention",
    )(q, qt, keys, values, lower_rel)


def passed_along(block, axis):
    n = lax.axis_size(axis)
    return lax.ppermute(block, axis, [(i, (i + 1) % n) for i in range(n)])


def body(
    queries, query_tangent, key_value, key_value_tangents, doc_lengths, out_weight, weight_tangent
):
    tokens = queries.shape[0]
    seq_index = lax.axis_index("seq")
    full_weight = lax.all_gather(out_weight, "seq", axis=0, tiled=True)
    full_tangent = lax.all_gather(weight_tangent, "seq", axis=0, tiled=True)
    stacked = jnp.concatenate(
        [key_value[:, 0], key_value_tangents[:, 0], key_value[:, 1], key_value_tangents[:, 1]],
        axis=1,
    )
    prior = passed_along(stacked[tokens - WINDOW :], "seq")
    context = jnp.concatenate([prior, stacked], axis=0)
    doc_ends = jnp.cumsum(doc_lengths)
    doc_starts = doc_ends - doc_lengths
    position = seq_index * tokens + jnp.arange(tokens, dtype=jnp.int32)
    doc_first = jnp.max(
        jnp.where(doc_starts[None, :] <= position[:, None], doc_starts[None, :], 0), axis=1
    )
    lower = jnp.maximum(doc_first, position - WINDOW + 1)
    lower_rel = lower - (position // STRETCH * STRETCH - WINDOW)
    lower_rel = jnp.broadcast_to(lower_rel[:, None], (tokens, 128))
    att, tan = attention(
        queries, query_tangent, context[:, : 2 * HEAD], context[:, 2 * HEAD :], lower_rel
    )
    part = jnp.dot(att, full_weight, preferred_element_type=jnp.float32).astype(jnp.bfloat16)
    part_tan = (
        jnp.dot(tan, full_weight, preferred_element_type=jnp.float32)
        + jnp.dot(att, full_tangent, preferred_element_type=jnp.float32)
    ).astype(jnp.bfloat16)
    return (
        lax.psum_scatter(part, "kv", scatter_dimension=1, tiled=True),
        lax.psum_scatter(part_tan, "kv", scatter_dimension=1, tiled=True),
    )


def solution(mesh):
    in_specs = (
        P("seq", "kv"),
        P("seq", "kv"),
        P("seq", None, "kv"),
        P("seq", None, "kv"),
        P(),
        P(("kv", "seq"), None),
        P(("kv", "seq"), None),
    )
    out_specs = (P("seq", "kv"), P("seq", "kv"))
    return jax.shard_map(body, mesh=mesh, in_specs=in_specs, out_specs=out_specs, check_vma=False)
```

time: 290 us -> 213 us (0.73)
  matrix products: 61.8 us -> 28.2 us
  other arithmetic: 24.6 us -> 0.96 us
  waiting for transfers between devices: 168 us -> 150 us
  Pallas kernels: 0 us -> 13.6 us
  local copies, waits for them, and re-layouts: 17.8 us -> 4.91 us
    reduce_scatter x2, waiting for transfers between devices: 151 us -> 89.1 us  [the longest x1 49.4 us: body(): lax.psum_scatter(part_tan, 'kv', scatter_dimension=1, tiled=True)]
    all_gather x2, waiting for transfers between devices: 16.9 us -> 51 us  [the longest x1 28.9 us: body(): full_tangent = lax.all_gather(weight_tangent, 'seq', axis=0, tiled=True)]
    dot_general x9 -> x3, matrix products: 61.8 us -> 28.2 us  [the longest x1 10.6 us: body(): jnp.dot(tan, full_weight, preferred_element_type=jnp.float32)]
    pallas_call x0 -> x1, Pallas kernels: none -> 13.6 us  [attention(): pl.pallas_call(functools.partial(attention_kernel, unroll), out_shape=(sh...]
    sub x2 -> x1, other arithmetic: 13 us -> 0.01 us  [body(): lower_rel = lower - (position // STRETCH * STRETCH - WINDOW)]
    unnamed x25 -> x10, local copies, waits for them, and re-layouts: 9.84 us -> 1.33 us
    ppermute x1, waiting for transfers between devices: 0.01 us -> 8.44 us  [passed_along(): return lax.ppermute(block, axis, [(i, (i + 1) % n) for i in range(n)])]
    convert_element_type x4 -> x0, other arithmetic: 5.47 us -> none  [the longest x2 5.39 us: body(): return (layer_out.astype(jnp.bfloat16), out_tangent.astype(jnp.bfloat16))]
  transfers between devices with their start and end apart: 5 -> 5, of which waited for: 3 -> 5; matrix products, arithmetic and copies ran while one was open for 30% -> 15% of each run, Pallas kernels for 0% -> 6%
where the time goes in v1:
time: 213 us; the launch traced here: 212 us
  waiting for transfers between devices  150 us (70%)
  matrix products  28.2 us (13%)
  between operations  13.9 us (7%)
  Pallas kernels  13.6 us (6%)
  local copies, waits for them, and re-layouts  4.91 us (2%)
    reduce_scatter x1, waiting for transfers between devices, body(): lax.psum_scatter(part_tan, 'kv', scatter_dimension=1, tiled=True)  49.4 us
    reduce_scatter x1, waiting for transfers between devices, body(): lax.psum_scatter(part, 'kv', scatter_dimension=1, tiled=True)  39.7 us
    all_gather x1, waiting for transfers between devices, body(): full_tangent = lax.all_gather(weight_tangent, 'seq', axis=0, tiled=True)  28.9 us
    all_gather x1, waiting for transfers between devices, body(): full_weight = lax.all_gather(out_weight, 'seq', axis=0, tiled=True)  22.1 us
    pallas_call x1, Pallas kernels, attention(): pl.pallas_call(functools.partial(attention_kernel, unroll), out_shape=(sh...  13.6 us
    dot_general x1, matrix products, body(): jnp.dot(tan, full_weight, preferred_element_type=jnp.float32)  10.6 us
    dot_general x1, matrix products, body(): jnp.dot(att, full_tangent, preferred_element_type=jnp.float32)  9.47 us
    ppermute x1, waiting for transfers between devices, passed_along(): return lax.ppermute(block, axis, [(i, (i + 1) % n) for i in range(n)])  8.44 us
  transfers between devices with their start and end apart: 5, of which 5 were waited for; matrix products, arithmetic and copies ran while one was open for 15% of the time, Pallas kernels for 6%

profile of v1, /device:TPU:0, one launch (start us, length us, event | category | flops | bytes accessed | tf_op | source)
XLA Modules:
  0.0 211.8 jit_solution(9706459696068352976)
XLA Ops:
  7.2 0.0 all-gather.3.cloned.1.call-start
  7.2 0.7 all-gather.3.cloned.1.call-update
  7.9 0.0 all-gather.5.cloned.1.call-start
  7.9 0.7 all-gather.5.cloned.1.call-update
  8.7 0.0 reduce-scatter.3.cloned.1.call-start
  8.7 2.2 %fusion.8 = (bf16[1024,1,128]{2,1,0:T(2,128)(2,1)S(1)}, bf16[1024,1,128]{2,1,0:T(2,128)(2,1)S(1)}) fusion(bf16[1024,2,128]{2,1,0:T(2,128)(2,1)} %param.10), kind=kLoop, calls=%fused_computation.27 | loop fusion | bytes 1048576 | tf_op jit(solution)/shard_map/slice | solution.py:95
  10.9 0.1 copy_bitcast_fusion
  11.0 0.0 copy-start.4
  11.0 0.7 fusion.7
  11.8 0.1 copy_bitcast_fusion.1
  11.9 0.1 collective-permute-start
  12.0 0.3 reduce-window.9
  12.3 0.1 slice.35
  12.4 0.1 slice_reduce_fusion
  12.5 0.1 bitcast_subtract_fusion
  12.6 0.4 select_reduce_fusion
  13.0 8.4 %collective-permute-done = bf16[224,512]{1,0:T(8,128)(2,1)S(1)} collective-permute-done((bf16[224,512]{1,0:T(8,128)(2,1)S(1)}, bf16[224,512]{1,0:T(8,128)(2,1)S(1)}, u32[]{:S(2)}, u32[]{:S(2)}) %collective-permute-start) | collective-permute-done | bytes 229408 | tf_op jit(solution)/shard_map/ppermute | solution.py:84
  21.5 0.1 maximum_maximum_fusion
  21.6 0.1 fusion.6
  21.7 0.2 broadcast_in_dim.13.lower_ref
  21.9 13.6 %attention.1 = (bf16[1024,1024]{1,0:T(8,128)(2,1)S(1)}, bf16[1024,1024]{1,0:T(8,128)(2,1)S(1)}) custom-call(bf16[1024,1024]{1,0:T(8,128)(2,1)S(1)} %copy-done, bf16[1024,1024]{1,0:T(8,128)(2,1)S(1)} %copy-done.1, bf16[1248,256]{1,0:T(8,128)(2,1)S(1)} %get-tuple-element.7.keys_ref, bf16[1248,256]{1,0:T(8,128)(2,1)S(1)} %get-tuple-element.6.values_ref, ...), custom_call_target="tpu_custom_call" | custom-call | tf_op jit(solution)/shard_map/attention/pallas_call | solution.py:72
  35.5 1.3 copy-done.2
  36.8 22.1 %all-gather.3.cloned.1.call-done = bf16[1024,2048]{1,0:T(8,128)(2,1)} async-done(((bf16[32,2048]{1,0:T(8,128)(2,1)}), bf16[1024,2048]{1,0:T(8,128)(2,1)}) %all-gather.3.cloned.1.call-update) | async-done | bytes 4194320 | tf_op jit(solution)/shard_map/all_gather | solution.py:92
  58.9 8.2 %convolution_convert_fusion = bf16[1024,2048]{1,0:T(8,128)(2,1)} fusion(bf16[1024,1024]{1,0:T(8,128)(2,1)S(1)} %get-tuple-element.4, bf16[1024,2048]{1,0:T(8,128)(2,1)} %all-gather.3.cloned.1.call-done), kind=kOutput, calls=%fused_computation.1 | convolution fusion | flops 4297064448 | bytes 10485760 | tf_op jit(solution)/shard_map/dot_general | solution.py:112
  67.1 0.0 reduce-scatter.3.cloned.1.call-update
  67.1 0.0 reduce-scatter.5.cloned.1.call-start
  67.2 10.6 %fusion.9 = f32[1024,2048]{1,0:T(8,128)} fusion(bf16[1024,1024]{1,0:T(8,128)(2,1)} %copy-done.2, bf16[1024,2048]{1,0:T(8,128)(2,1)} %all-gather.3.cloned.1.call-done), kind=kOutput, calls=%fused_computation.28 | convolution fusion | flops 4294967296 | bytes 14680064 | tf_op jit(solution)/shard_map/dot_general | solution.py:114
  77.8 28.9 %all-gather.5.cloned.1.call-done = bf16[1024,2048]{1,0:T(8,128)(2,1)} async-done(((bf16[32,2048]{1,0:T(8,128)(2,1)}), bf16[1024,2048]{1,0:T(8,128)(2,1)}) %all-gather.5.cloned.1.call-update) | async-done | bytes 4194320 | tf_op jit(solution)/shard_map/all_gather | solution.py:93
  106.7 9.5 %add_convert_fusion = bf16[1024,2048]{1,0:T(8,128)(2,1)} fusion(f32[1024,2048]{1,0:T(8,128)} %fusion.9, bf16[1024,1024]{1,0:T(8,128)(2,1)S(1)} %get-tuple-element.4, bf16[1024,2048]{1,0:T(8,128)(2,1)} %all-gather.5.cloned.1.call-done), kind=kOutput, calls=%fused_computation | convolution fusion | flops 4299161600 | bytes 18874368 | tf_op jit(solution)/shard_map/dot_general | solution.py:115
  116.1 0.0 reduce-scatter.5.cloned.1.call-update
  116.2 39.7 %reduce-scatter.3.cloned.1.call-done = bf16[1024,512]{1,0:T(8,128)(2,1)} async-done(((bf16[1024,2048]{1,0:T(8,128)(2,1)}), bf16[1024,512]{1,0:T(8,128)(2,1)}) %reduce-scatter.3.cloned.1.call-update) | async-done | bytes 1048592 | tf_op jit(solution)/shard_map/reduce_scatter | solution.py:118
  155.8 49.4 %reduce-scatter.5.cloned.1.call-done = bf16[1024,512]{1,0:T(8,128)(2,1)} async-done(((bf16[1024,2048]{1,0:T(8,128)(2,1)}), bf16[1024,512]{1,0:T(8,128)(2,1)}) %reduce-scatter.5.cloned.1.call-update) | async-done | bytes 1048592 | tf_op jit(solution)/shard_map/reduce_scatter | solution.py:119
  (12 shorter events, 0.1 us)
Async XLA Ops:
  7.2 3.9 %copy-start.3 = (bf16[1024,2,128]{2,1,0:T(2,128)(2,1)S(1)}, bf16[1024,2,128]{2,1,0:T(2,128)(2,1)}, u32[]{:S(2)}) copy-start(bf16[1024,2,128]{2,1,0:T(2,128)(2,1)} %param.9) | copy-start | bytes 1572868
  7.2 51.8 %all-gather.3.cloned.1.call-start = ((), (), s32[]{:S(2)}) async-start(), calls=%async_computation.2 | async-start | bytes 4325376 | tf_op jit(solution)/shard_map/all_gather | solution.py:92
  7.9 98.8 %all-gather.5.cloned.1.call-start = ((), (), s32[]{:S(2)}) async-start(), calls=%async_computation.4 | async-start | bytes 4325376 | tf_op jit(solution)/shard_map/all_gather | solution.py:93
  8.7 147.2 %reduce-scatter.3.cloned.1.call-start = ((), (), s32[]{:S(2)}) async-start(), calls=%async_computation.3 | async-start | bytes 5242880 | tf_op jit(solution)/shard_map/reduce_scatter | solution.py:118
  11.0 1.0 copy-start.4
  11.9 9.6 %collective-permute-start = (bf16[224,512]{1,0:T(8,128)(2,1)S(1)}, bf16[224,512]{1,0:T(8,128)(2,1)S(1)}, u32[]{:S(2)}, u32[]{:S(2)}) collective-permute-start(bf16[224,512]{1,0:T(8,128)(2,1)S(1)} %pad_maximum_fusion), channel_id=1, source_target_pairs={{0,1},{1,2},{2,3},{3,4},{4,5},{5,6},{6,7},{7,8},{8,9},{9,10},{10,1... | collective-permute-start | bytes 688136 | tf_op jit(solution)/shard_map/ppermute | solution.py:84
  13.0 8.9 %copy-start = (bf16[1024,1024]{1,0:T(8,128)(2,1)S(1)}, bf16[1024,1024]{1,0:T(8,128)(2,1)}, u32[]{:S(2)}) copy-start(bf16[1024,1024]{1,0:T(8,128)(2,1)} %q_ref.1) | copy-start | bytes 6291460
  13.0 8.9 %copy-start.1 = (bf16[1024,1024]{1,0:T(8,128)(2,1)S(1)}, bf16[1024,1024]{1,0:T(8,128)(2,1)}, u32[]{:S(2)}) copy-start(bf16[1024,1024]{1,0:T(8,128)(2,1)} %qt_ref.1) | copy-start | bytes 6291460
  35.5 1.3 copy-start.2
  67.1 138.1 %reduce-scatter.5.cloned.1.call-start = ((), (), s32[]{:S(2)}) async-start(), calls=%async_computation.5 | async-start | bytes 5242880 | tf_op jit(solution)/shard_map/reduce_scatter | solution.py:119
Sparse Core Ops, SparseCore 0:
  10.2 48.6 all-gather.2
  61.2 45.4 all-gather.4
  109.7 46.1 reduce-scatter.2
  158.7 46.5 reduce-scatter.4

commit v2 on v1

v2 whole, which is shorter than its diff:
```python
import math

import jax
import jax.numpy as jnp
from jax import lax
from jax.experimental import pallas as pl
from jax.experimental.pallas import tpu as pltpu
from jax.sharding import PartitionSpec as P

STRETCH = 32
WINDOW = 224
HEAD = 128
HEADS = 8
SPAN = WINDOW + STRETCH
MASKED = -1e30
SCALE = 1.0 / math.sqrt(HEAD)
EXP_SCALE = SCALE * math.log2(math.e)
MESH = pl.DeviceIdType.MESH

TOKENS = 1024
NDOCS = 256
GROUP = HEADS * HEAD
SHARE = 512
BLOCK = 256
BLOCKS = TOKENS // BLOCK
PAIR = 2 * STRETCH
STEPS = TOKENS // PAIR
RING = 4
ROWS = 32


def attend_block(q, qt, keys, values, starts, position):
    rows = STRETCH * HEADS
    qs = jnp.concatenate([q[:, HEAD * h : HEAD * (h + 1)] for h in range(HEADS)], axis=0)
    qts = jnp.concatenate([qt[:, HEAD * h : HEAD * (h + 1)] for h in range(HEADS)], axis=0)
    dims = (((1,), (1,)), ((), ()))
    s = lax.dot_general(qs, keys[:, :HEAD], dims, preferred_element_type=jnp.float32)
    t = lax.dot_general(
        jnp.concatenate([qts, qs], axis=1), keys, dims, preferred_element_type=jnp.float32
    )
    row = lax.broadcasted_iota(jnp.int32, (STRETCH, SPAN), 0)
    column = lax.broadcasted_iota(jnp.int32, (STRETCH, SPAN), 1)
    here = (position + row).astype(jnp.float32)
    first = jnp.max(jnp.where(starts <= here, starts, 0.0), axis=-1, keepdims=True)
    there = (position - WINDOW + column).astype(jnp.float32)
    admitted = (there >= first) & (there <= here) & (there > here - WINDOW)
    s = jnp.where(admitted[None], s.reshape(HEADS, STRETCH, SPAN), MASKED).reshape(rows, SPAN)
    peak = jnp.max(s, axis=-1, keepdims=True)
    e = jnp.exp2((s - peak) * EXP_SCALE)
    prob = e * (1.0 / jnp.sum(e, axis=-1, keepdims=True))
    t = t * SCALE
    mean = jnp.sum(prob * t, axis=-1, keepdims=True)
    prob_t = prob * (t - mean)
    flat = (((1,), (0,)), ((), ()))
    pv = lax.dot_general(prob.astype(jnp.bfloat16), values, flat, preferred_element_type=jnp.float32)
    tv = lax.dot_general(
        prob_t.astype(jnp.bfloat16), values[:, :HEAD], flat, preferred_element_type=jnp.float32
    )
    return pv[:, :HEAD].astype(jnp.bfloat16), (tv + pv[:, HEAD:]).astype(jnp.bfloat16)


def doc_starts(lengths):
    lane = lax.broadcasted_iota(jnp.int32, (8, NDOCS), 1)
    own = jnp.broadcast_to(lengths, (8, NDOCS))
    total = own
    shift = 1
    while shift < NDOCS:
        total = total + jnp.where(lane >= shift, pltpu.roll(total, shift, 1), 0)
        shift *= 2
    return (total - own).astype(jnp.float32)[:1]


def layer_kernel(
    lengths_ref, q_hbm, qt_hbm, kv_hbm, w_hbm, wt_hbm, out_hbm, tan_hbm,
    q_ref, qt_ref, ctx, w_ref, aa, d_out, d_in, m_out, m_in, own, final,
    load_sem, store_sem, halo_sem,
    one_send, one_recv, two_send, two_recv, three_send, three_recv, core_send, core_recv,
    d_send, d_recv, m_send, m_recv,
):
    y = lax.axis_index("kv")
    s = lax.axis_index("seq")
    z, x, c = s // 8, (s // 2) % RING, s % 2

    def seat(zz, xx, cc):
        return (y, lax.rem(zz, RING) * 8 + lax.rem(xx, RING) * 2 + cc)

    right, left = (lax.rem(y + 1, RING), s), (lax.rem(y + 3, RING), s)
    after, before = (y, lax.rem(s + 1, 32)), (y, lax.rem(s + 31, 32))
    partner = seat(z, x, 1 - c)

    def along(axis, distance):
        return seat(z, x + distance, c) if axis == 0 else seat(z + distance, x, c)

    loads = [
        pltpu.make_async_copy(kv_hbm, ctx.at[:, pl.ds(WINDOW, TOKENS)], load_sem.at[0]),
        pltpu.make_async_copy(q_hbm, q_ref, load_sem.at[1]),
        pltpu.make_async_copy(qt_hbm, qt_ref, load_sem.at[2]),
    ]
    for n in range(RING):
        share = lax.rem(y + (2, 1, 3, 0)[n], RING)
        columns = pl.ds(pl.multiple_of(share * SHARE, SHARE), SHARE)
        loads.append(
            pltpu.make_async_copy(w_hbm.at[:, columns], w_ref.at[n, 0, z, x, c], load_sem.at[3 + n])
        )
        loads.append(
            pltpu.make_async_copy(wt_hbm.at[:, columns], w_ref.at[n, 1, z, x, c], load_sem.at[7 + n])
        )
    for load in loads:
        load.start()

    barrier = pltpu.get_barrier_semaphore()
    greeted = [along(a, d) for a in (0, 1) for d in (1, 2, 3)]
    greeted += [partner, right, left, after, before]
    for device in greeted:
        pl.semaphore_signal(barrier, inc=1, device_id=device, device_id_type=MESH)
    pl.semaphore_wait(barrier, len(greeted))

    def remote(src, dst, send, recv, device):
        return pltpu.make_async_remote_copy(
            src_ref=src, dst_ref=dst, send_sem=send, recv_sem=recv,
            device_id=device, device_id_type=MESH,
        )

    def one(n, half):
        piece = w_ref.at[n, half, z, x, c]
        return [
            remote(piece, piece, one_send.at[n, half, d - 1], one_recv.at[n, half, d - 1],
                   along(half, d))
            for d in (1, 2, 3)
        ]

    def line(n, half, k, start=0, size=RING):
        part = pl.ds(start, size)
        return w_ref.at[n, 0, k, part, c] if half == 0 else w_ref.at[n, 1, part, k, c]

    def place(half):
        return z if half == 0 else x

    def two(n, half):
        mine = line(n, half, place(half))
        return [
            remote(mine, mine, two_send.at[n, half, j], two_recv.at[n, half, j],
                   along(1 - half, (1, 3)[j]))
            for j in (0, 1)
        ]

    def three(n, half):
        copies = []
        for j in (0, 1):
            k = lax.rem(place(half) + (3, 1)[j], RING)
            piece = line(n, half, k, 2 * j, 2)
            copies.append(
                remote(piece, piece, three_send.at[n, half, j], three_recv.at[n, half, j],
                       along(1 - half, (1, 3)[j]))
            )
        return copies

    def core(n, half, j):
        piece = line(n, half, lax.rem(place(half) + j, RING))
        return remote(piece, piece, core_send.at[n, half, j], core_recv.at[n, half, j], partner)

    halo = remote(
        kv_hbm.at[:, pl.ds(TOKENS - WINDOW, WINDOW)], ctx.at[:, pl.ds(0, WINDOW)],
        halo_sem.at[0], halo_sem.at[1], after,
    )

    def weights_one(n):
        for half in (0, 1):
            loads[3 + 2 * n + half].wait()
            for copy in one(n, half):
                copy.start()

    def weights_two(n):
        for half in (0, 1):
            for copy in one(n, half):
                copy.wait_recv()
            for copy in two(n, half):
                copy.start()
            core(n, half, 0).start()

    def weights_three(n):
        for half in (0, 1):
            for copy in two(n, half):
                copy.wait_recv()
            for copy in three(n, half):
                copy.start()
            core(n, half, 1).start()
            core(n, half, 3).start()

    def weights_four(n):
        for half in (0, 1):
            for copy in three(n, half):
                copy.wait_recv()
            core(n, half, 2).start()

    def weights_ready(n):
        for half in (0, 1):
            for j in range(RING):
                core(n, half, j).wait_recv()

    weights_one(0)
    halo.start()
    starts = doc_starts(lengths_ref[...])
    loads[0].wait()
    loads[1].wait()
    loads[2].wait()

    def order(b):
        return lax.rem(b + 1, BLOCKS)

    def attend_pair(i):
        for k in (0, 1):
            at = pl.multiple_of(lax.rem(i * PAIR + BLOCK, TOKENS) + k * STRETCH, STRETCH)
            here = pl.ds(at, STRETCH)
            span = pl.ds(at, SPAN)
            out, tan = attend_block(
                q_ref[here, :], qt_ref[here, :], ctx[0, span, :], ctx[1, span, :],
                starts, s * TOKENS + at,
            )
            for h in range(HEADS):
                rows = slice(STRETCH * h, STRETCH * (h + 1))
                aa[here, HEAD * h : HEAD * (h + 1)] = tan[rows]
                aa[here, GROUP + HEAD * h : GROUP + HEAD * (h + 1)] = out[rows]

    def project(b, n, put):
        here = pl.ds(pl.multiple_of(b * BLOCK, BLOCK), BLOCK)

        def tile(j, carry):
            columns = pl.ds(pl.multiple_of(j * 256, 256), 256)
            w = w_ref[n, 0, :, :, :, :, columns].reshape(GROUP, 256)
            wt = w_ref[n, 1, :, :, :, :, columns].reshape(GROUP, 256)
            att = aa[here, GROUP:]
            value = jnp.dot(att, w, preferred_element_type=jnp.float32)
            tan = jnp.dot(aa[here, :GROUP], w, preferred_element_type=jnp.float32)
            tan = tan + jnp.dot(att, wt, preferred_element_type=jnp.float32)
            put(columns, value, tan)
            return carry

        lax.fori_loop(0, SHARE // 256, tile, 0)

    def d_copy(b, j):
        return remote(d_out.at[b, j], d_in.at[b, j], d_send.at[b, j], d_recv.at[b, j],
                      (right, left)[j])

    def m_copy(b, j):
        return remote(m_out.at[b, j], m_in.at[b, j], m_send.at[b, j], m_recv.at[b, j],
                      (right, left)[j])

    def far(b):
        def put(columns, value, tan):
            d_out[b, 0, :, columns] = value.astype(jnp.bfloat16)
            d_out[b, 1, :, columns] = tan.astype(jnp.bfloat16)

        project(b, 0, put)
        d_copy(b, 0).start()
        d_copy(b, 1).start()

    def near(b, j):
        d_copy(b, j).wait_recv()

        def put(columns, value, tan):
            came = d_in[b, j, :, columns].astype(jnp.float32)
            if j == 0:
                value = value + came
            else:
                tan = tan + came
            m_out[b, j, 0, :, columns] = value.astype(jnp.bfloat16)
            m_out[b, j, 1, :, columns] = tan.astype(jnp.bfloat16)

        project(b, 1 + j, put)
        m_copy(b, j).start()

    def home(b):
        def put(columns, value, tan):
            own[b, 0, :, columns] = value
            own[b, 1, :, columns] = tan

        project(b, 3, put)

    def step(i, carry):
        @pl.when(i == 12)
        def _():
            halo.wait_recv()

        attend_pair(i)
        for n in range(RING):
            @pl.when(i == 3 * n + 1)
            def _():
                weights_two(n)
                if n + 1 < RING:
                    weights_one(n + 1)

            @pl.when(i == 3 * n + 4)
            def _():
                weights_three(n)

            @pl.when(i == min(3 * n + 6, STEPS - 1))
            def _():
                weights_four(n)

        return carry

    lax.fori_loop(0, STEPS, step, 0)
    weights_ready(0)

    def far_step(b, carry):
        far(order(b))
        return carry

    lax.fori_loop(0, BLOCKS, far_step, 0)
    weights_ready(1)
    weights_ready(2)

    def near_step(b, carry):
        near(order(b), 0)
        near(order(b), 1)
        return carry

    lax.fori_loop(0, BLOCKS, near_step, 0)
    weights_ready(3)

    def home_step(b, carry):
        home(order(b))
        return carry

    lax.fori_loop(0, BLOCKS, home_step, 0)

    def stores(b):
        here = pl.ds(pl.multiple_of(b * BLOCK, BLOCK), BLOCK)
        return [
            pltpu.make_async_copy(final.at[b, k], (out_hbm, tan_hbm)[k].at[here], store_sem.at[b, k])
            for k in (0, 1)
        ]

    def last_step(b, carry):
        b = order(b)
        m_copy(b, 0).wait_recv()
        m_copy(b, 1).wait_recv()
        for k in (0, 1):
            final[b, k] = (
                own[b, k]
                + m_in[b, 0, k].astype(jnp.float32)
                + m_in[b, 1, k].astype(jnp.float32)
            ).astype(jnp.bfloat16)
        for copy in stores(b):
            copy.start()
        return carry

    lax.fori_loop(0, BLOCKS, last_step, 0)

    def drain(b, carry):
        for j in (0, 1):
            d_copy(b, j).wait_send()
            m_copy(b, j).wait_send()
        for copy in stores(b):
            copy.wait()
        return carry

    lax.fori_loop(0, BLOCKS, drain, 0)
    halo.wait_send()
    for n in range(RING):
        for half in (0, 1):
            for copy in one(n, half) + two(n, half) + three(n, half):
                copy.wait_send()
            for j in range(RING):
                core(n, half, j).wait_send()


def layer(lengths, q, qt, kv, w, wt):
    anywhere = pl.BlockSpec(memory_space=pl.ANY)
    shape = jax.ShapeDtypeStruct((TOKENS, SHARE), jnp.bfloat16)
    bf16, f32 = jnp.bfloat16, jnp.float32
    dma = pltpu.SemaphoreType.DMA
    return pl.pallas_call(
        layer_kernel,
        out_shape=(shape, shape),
        in_specs=[pl.BlockSpec(memory_space=pltpu.VMEM)] + [anywhere] * 5,
        out_specs=(anywhere, anywhere),
        scratch_shapes=[
            pltpu.VMEM((TOKENS, GROUP), bf16),
            pltpu.VMEM((TOKENS, GROUP), bf16),
            pltpu.VMEM((2, WINDOW + TOKENS, 2 * HEAD), bf16),
            pltpu.VMEM((RING, 2, RING, RING, 2, ROWS, SHARE), bf16),
            pltpu.VMEM((TOKENS, 2 * GROUP), bf16),
            pltpu.VMEM((BLOCKS, 2, BLOCK, SHARE), bf16),
            pltpu.VMEM((BLOCKS, 2, BLOCK, SHARE), bf16),
            pltpu.VMEM((BLOCKS, 2, 2, BLOCK, SHARE), bf16),
            pltpu.VMEM((BLOCKS, 2, 2, BLOCK, SHARE), bf16),
            pltpu.VMEM((BLOCKS, 2, BLOCK, SHARE), f32),
            pltpu.VMEM((BLOCKS, 2, BLOCK, SHARE), bf16),
            dma((11,)),
            dma((BLOCKS, 2)),
            dma((2,)),
            dma((RING, 2, 3)),
            dma((RING, 2, 3)),
            dma((RING, 2, 2)),
            dma((RING, 2, 2)),
            dma((RING, 2, 2)),
            dma((RING, 2, 2)),
            dma((RING, 2, RING)),
            dma((RING, 2, RING)),
            dma((BLOCKS, 2)),
            dma((BLOCKS, 2)),
            dma((BLOCKS, 2)),
            dma((BLOCKS, 2)),
        ],
        compiler_params=pltpu.CompilerParams(
            collective_id=0, has_side_effects=True, vmem_limit_bytes=58 << 20
        ),
        name="layer",
    )(lengths, q, qt, kv, w, wt)


def body(
    queries, query_tangent, key_value, key_value_tangents, doc_lengths, out_weight, weight_tangent
):
    context = jnp.stack(
        [
            jnp.concatenate([key_value[:, k], key_value_tangents[:, k]], axis=1)
            for k in (0, 1)
        ]
    )
    return layer(
        doc_lengths[None, :], queries, query_tangent, context, out_weight, weight_tangent
    )


def solution(mesh):
    in_specs = (
        P("seq", "kv"),
        P("seq", "kv"),
        P("seq", None, "kv"),
        P("seq", None, "kv"),
        P(),
        P(("kv", "seq"), None),
        P(("kv", "seq"), None),
    )
    out_specs = (P("seq", "kv"), P("seq", "kv"))
    return jax.shard_map(body, mesh=mesh, in_specs=in_specs, out_specs=out_specs, check_vma=False)
```

time: 213 us -> 120 us (0.56)
  waiting for transfers between devices: 150 us -> 0 us
  Pallas kernels: 13.6 us -> 112 us
  matrix products: 28.2 us -> 0 us
  between operations: 13.9 us -> 0.69 us
    pallas_call x1, Pallas kernels: 13.6 us -> 112 us  [layer(): pl.pallas_call(layer_kernel, out_shape=(shape, shape), in_specs=[pl.Block...]
    reduce_scatter x2 -> x0, waiting for transfers between devices: 89.1 us -> none  [the longest x1 49.4 us: body(): lax.psum_scatter(part_tan, 'kv', scatter_dimension=1, tiled=True)]
    all_gather x2 -> x0, waiting for transfers between devices: 51 us -> none  [the longest x1 28.9 us: body(): full_tangent = lax.all_gather(weight_tangent, 'seq', axis=0, tiled=True)]
    dot_general x3 -> x0, matrix products: 28.2 us -> none  [the longest x1 10.6 us: body(): jnp.dot(tan, full_weight, preferred_element_type=jnp.float32)]
    ppermute x1 -> x0, waiting for transfers between devices: 8.44 us -> none  [passed_along(): return lax.ppermute(block, axis, [(i, (i + 1) % n) for i in range(n)])]
  transfers between devices with their start and end apart: 5 -> 0, of which waited for: 5 -> 0; matrix products, arithmetic and copies ran while one was open for 15% -> 0% of each run, Pallas kernels for 6% -> 0%
where the time goes in v2:
time: 120 us
  Pallas kernels  112 us (93%)
  local copies, waits for them, and re-layouts  6.38 us (5%)
  other arithmetic  1.22 us (1%)
    pallas_call x1, Pallas kernels, layer(): pl.pallas_call(layer_kernel, out_shape=(shape, shape), in_specs=[pl.Block...  112 us
    unnamed x6, local copies, waits for them, and re-layouts  3.33 us

profile of v2, /device:TPU:0, one launch (start us, length us, event | category | flops | bytes accessed | tf_op | source)
XLA Modules:
  0.0 119.9 jit_solution(8342501932704296658)
XLA Ops:
  0.6 0.0 copy-start
  0.6 2.2 %fusion = (bf16[1024,1,128]{2,1,0:T(2,128)(2,1)S(1)}, bf16[1024,1,128]{2,1,0:T(2,128)(2,1)S(1)}) fusion(bf16[1024,2,128]{2,1,0:T(2,128)(2,1)} %param.9), kind=kLoop, calls=%fused_computation.7 | loop fusion | bytes 1048576 | tf_op jit(solution)/shard_map/slice | solution.py:419
  2.8 0.1 copy_bitcast_fusion.1
  2.9 0.0 copy-done
  2.9 0.7 fusion.1
  3.6 0.1 copy_bitcast_fusion
  3.7 0.1 maximum_bitcast_fusion.1
  3.8 0.1 maximum_bitcast_fusion
  3.9 1.1 pad_maximum_fusion.kv_hbm
  5.0 111.6 %layer.1 = (bf16[1024,512]{1,0:T(8,128)(2,1)}, bf16[1024,512]{1,0:T(8,128)(2,1)}) custom-call(s32[1,256]{1,0:T(1,128)} %bitcast.13, bf16[1024,1024]{1,0:T(8,128)(2,1)} %q_hbm.1, bf16[1024,1024]{1,0:T(8,128)(2,1)} %qt_hbm.1, bf16[2,1024,256]{2,1,0:T(8,128)(2,1)} %pad_maximum_fusion.kv_hbm, bf16[32,2048]{1,0:T(8,128)(2,1)} %w_hbm.1, bf16[32,2048]{1,0:T(8,128)(2,1)} %wt_hbm.1), custom_call_target="tpu_custom_call" | custom-call | tf_op jit(solution)/shard_map/layer/pallas_call | solution.py:374
  116.5 0.0 copy-start.1
  116.5 2.4 %copy.23 = bf16[1024,512]{1,0:T(8,128)(2,1)} copy(bf16[1024,512]{1,0:T(8,128)(2,1)} %get-tuple-element.12) | data formatting | bytes 2097152
  118.9 0.0 copy-done.1
  118.9 1.0 copy.24
Async XLA Ops:
  0.6 2.3 %copy-start = (bf16[1024,2,128]{2,1,0:T(2,128)(2,1)S(1)}, bf16[1024,2,128]{2,1,0:T(2,128)(2,1)}, u32[]{:S(2)}) copy-start(bf16[1024,2,128]{2,1,0:T(2,128)(2,1)} %param.10) | copy-start | bytes 1572868
  116.5 2.4 %copy-start.1 = (bf16[1024,512]{1,0:T(8,128)(2,1)S(1)}, bf16[1024,512]{1,0:T(8,128)(2,1)}, u32[]{:S(2)}) copy-start(bf16[1024,512]{1,0:T(8,128)(2,1)} %get-tuple-element.13) | copy-start | bytes 3145732

commit v3 on v2

v3 whole, which is shorter than its diff:
```python
import functools
import math

import jax
import jax.numpy as jnp
from jax import lax
from jax.experimental import pallas as pl
from jax.experimental.pallas import tpu as pltpu
from jax.sharding import PartitionSpec as P

STRETCH = 32
WINDOW = 224
HEAD = 128
HEADS = 8
SPAN = WINDOW + STRETCH
MASKED = -1e30
SCALE = 1.0 / math.sqrt(HEAD)
EXP_SCALE = SCALE * math.log2(math.e)
MESH = pl.DeviceIdType.MESH

TOKENS = 1024
NDOCS = 256
GROUP = HEADS * HEAD
SHARE = 512
BLOCK = 256
BLOCKS = TOKENS // BLOCK
PAIR = 2 * STRETCH
STEPS = TOKENS // PAIR
RING = 4
ROWS = 32
PART = 256
PARTS = SHARE // PART
PIECES = RING * PARTS
VMEM_LIMIT = 44 << 20


def attend_block(q, qt, keys, values, starts, position):
    rows = STRETCH * HEADS
    qs = jnp.concatenate([q[:, HEAD * h : HEAD * (h + 1)] for h in range(HEADS)], axis=0)
    qts = jnp.concatenate([qt[:, HEAD * h : HEAD * (h + 1)] for h in range(HEADS)], axis=0)
    dims = (((1,), (1,)), ((), ()))
    s = lax.dot_general(qs, keys[:, :HEAD], dims, preferred_element_type=jnp.float32)
    t = lax.dot_general(
        jnp.concatenate([qts, qs], axis=1), keys, dims, preferred_element_type=jnp.float32
    )
    row = lax.broadcasted_iota(jnp.int32, (STRETCH, SPAN), 0)
    column = lax.broadcasted_iota(jnp.int32, (STRETCH, SPAN), 1)
    here = (position + row).astype(jnp.float32)
    first = jnp.max(jnp.where(starts <= here, starts, 0.0), axis=-1, keepdims=True)
    there = (position - WINDOW + column).astype(jnp.float32)
    admitted = (there >= first) & (there <= here) & (there > here - WINDOW)
    s = jnp.where(admitted[None], s.reshape(HEADS, STRETCH, SPAN), MASKED).reshape(rows, SPAN)
    peak = jnp.max(s, axis=-1, keepdims=True)
    e = jnp.exp2((s - peak) * EXP_SCALE)
    prob = e * (1.0 / jnp.sum(e, axis=-1, keepdims=True))
    t = t * SCALE
    mean = jnp.sum(prob * t, axis=-1, keepdims=True)
    prob_t = prob * (t - mean)
    flat = (((1,), (0,)), ((), ()))
    pv = lax.dot_general(prob.astype(jnp.bfloat16), values, flat, preferred_element_type=jnp.float32)
    tv = lax.dot_general(
        prob_t.astype(jnp.bfloat16), values[:, :HEAD], flat, preferred_element_type=jnp.float32
    )
    return pv[:, :HEAD].astype(jnp.bfloat16), (tv + pv[:, HEAD:]).astype(jnp.bfloat16)


def doc_starts(lengths):
    lane = lax.broadcasted_iota(jnp.int32, (8, NDOCS), 1)
    own = jnp.broadcast_to(lengths, (8, NDOCS))
    total = own
    shift = 1
    while shift < NDOCS:
        total = total + jnp.where(lane >= shift, pltpu.roll(total, shift, 1), 0)
        shift *= 2
    return (total - own).astype(jnp.float32)[:1]


def layer_kernel(
    lengths_ref, q_hbm, qt_hbm, kv_hbm, kvt_hbm, w_hbm, wt_hbm, out_ref, tan_ref,
    q_ref, qt_ref, raw, wide, ctx, w_ref, aa, d_out, d_in, m_out, m_in, own,
    load_sem, halo_sem, one_send, one_recv, two_send, two_recv, core_send, core_recv,
    d_send, d_recv, m_send, m_recv,
):
    y = lax.axis_index("kv")
    s = lax.axis_index("seq")
    z, x, c = s // 8, (s // 2) % RING, s % 2

    def seat(zz, xx, cc):
        return (y, lax.rem(zz, RING) * 8 + lax.rem(xx, RING) * 2 + cc)

    right, left = (lax.rem(y + 1, RING), s), (lax.rem(y + 3, RING), s)
    after, before = (y, lax.rem(s + 1, 32)), (y, lax.rem(s + 31, 32))
    partner = seat(z, x, 1 - c)

    def along(axis, distance):
        return seat(z, x + distance, c) if axis == 0 else seat(z + distance, x, c)

    def w_loads(n):
        share = lax.rem(y + (2, 1, 3, 0)[n // PARTS], RING)
        columns = pl.ds(pl.multiple_of(share * SHARE + n % PARTS * PART, PART), PART)
        return [
            pltpu.make_async_copy(w_hbm.at[:, columns], w_ref.at[n, 0, z, x, c], load_sem.at[4 + n]),
            pltpu.make_async_copy(
                wt_hbm.at[:, columns], w_ref.at[n, 1, z, x, c], load_sem.at[4 + PIECES + n]
            ),
        ]

    tail = pl.ds(2 * WINDOW, 2 * TOKENS)
    loads = [
        pltpu.make_async_copy(kv_hbm, raw.at[0, tail], load_sem.at[0]),
        pltpu.make_async_copy(kvt_hbm, raw.at[1, tail], load_sem.at[1]),
        pltpu.make_async_copy(q_hbm, q_ref, load_sem.at[2]),
        pltpu.make_async_copy(qt_hbm, qt_ref, load_sem.at[3]),
    ]
    for load in w_loads(0) + w_loads(1) + loads:
        load.start()
    for n in range(2, PIECES):
        for load in w_loads(n):
            load.start()

    barrier = pltpu.get_barrier_semaphore()
    greeted = [along(a, d) for a in (0, 1) for d in (1, 2, 3)]
    greeted += [partner, right, left, after, before]
    for device in greeted:
        pl.semaphore_signal(barrier, inc=1, device_id=device, device_id_type=MESH)
    pl.semaphore_wait(barrier, len(greeted))

    def remote(src, dst, send, recv, device):
        return pltpu.make_async_remote_copy(
            src_ref=src, dst_ref=dst, send_sem=send, recv_sem=recv,
            device_id=device, device_id_type=MESH,
        )

    def one(n, half):
        piece = w_ref.at[n, half, z, x, c]
        return [
            remote(piece, piece, one_send.at[n, half, d - 1], one_recv.at[n, half, d - 1],
                   along(half, d))
            for d in (1, 3, 2)
        ]

    def two(n, half):
        line = w_ref.at[n, 0, z, :, c] if half == 0 else w_ref.at[n, 1, :, x, c]
        return [
            remote(line, line, two_send.at[n, half, d - 1], two_recv.at[n, half, d - 1],
                   along(1 - half, d))
            for d in (1, 3, 2)
        ]

    def core(n):
        mine = w_ref.at[n, :, :, :, c]
        return remote(mine, mine, core_send.at[n], core_recv.at[n], partner)

    def weights_one(n):
        for load in w_loads(n):
            load.wait()
        for half in (0, 1):
            for copy in one(n, half):
                copy.start()

    def weights_two(n):
        for half in (0, 1):
            for copy in one(n, half):
                copy.wait_recv()
            for copy in two(n, half):
                copy.start()

    def weights_core(n):
        for half in (0, 1):
            for copy in two(n, half):
                copy.wait_recv()
        core(n).start()

    def weights_ready(n):
        core(n).wait_recv()

    def halo(k):
        return remote(
            (kv_hbm, kvt_hbm)[k].at[pl.ds(2 * (TOKENS - WINDOW), 2 * WINDOW)],
            raw.at[k, pl.ds(0, 2 * WINDOW)], halo_sem.at[k, 0], halo_sem.at[k, 1], after,
        )

    weights_one(0)
    weights_one(1)
    halo(0).start()
    halo(1).start()
    starts = doc_starts(lengths_ref[...])

    def unpack(at, rows):
        for k in (0, 1):
            wide[k, : 2 * rows] = raw[k, pl.ds(2 * at, 2 * rows)].astype(jnp.float32)
            for j in (0, 1):
                ctx[j, pl.ds(at, rows), HEAD * k : HEAD * (k + 1)] = wide[
                    k, pl.ds(j, rows, stride=2), :
                ].astype(jnp.bfloat16)

    loads[0].wait()
    loads[1].wait()

    def unpack_step(i, carry):
        unpack(pl.multiple_of(WINDOW + i * 128, 32), 128)
        return carry

    lax.fori_loop(0, TOKENS // 128, unpack_step, 0)
    loads[2].wait()
    loads[3].wait()

    def order(b):
        return lax.rem(b + 1, BLOCKS)

    def attend_pair(i):
        for k in (0, 1):
            at = pl.multiple_of(lax.rem(i * PAIR + BLOCK, TOKENS) + k * STRETCH, STRETCH)
            here = pl.ds(at, STRETCH)
            span = pl.ds(at, SPAN)
            out, tan = attend_block(
                q_ref[here, :], qt_ref[here, :], ctx[0, span, :], ctx[1, span, :],
                starts, s * TOKENS + at,
            )
            for h in range(HEADS):
                rows = slice(STRETCH * h, STRETCH * (h + 1))
                aa[here, HEAD * h : HEAD * (h + 1)] = tan[rows]
                aa[here, GROUP + HEAD * h : GROUP + HEAD * (h + 1)] = out[rows]

    def project(b, n):
        here = pl.ds(pl.multiple_of(b * BLOCK, BLOCK), BLOCK)
        w = w_ref[n, 0].reshape(GROUP, PART)
        wt = w_ref[n, 1].reshape(GROUP, PART)
        att = aa[here, GROUP:]
        value = jnp.dot(att, w, preferred_element_type=jnp.float32)
        tan = jnp.dot(aa[here, :GROUP], w, preferred_element_type=jnp.float32)
        tan = tan + jnp.dot(att, wt, preferred_element_type=jnp.float32)
        return value, tan

    def d_copy(b, p, j):
        return remote(d_out.at[b, p, j], d_in.at[b, p, j], d_send.at[b, p, j], d_recv.at[b, p, j],
                      (right, left)[j])

    def m_copy(b, p, j):
        return remote(m_out.at[b, p, j], m_in.at[b, p, j], m_send.at[b, p, j], m_recv.at[b, p, j],
                      (right, left)[j])

    def far(b, p):
        value, tan = project(b, p)
        d_out[b, p, 0] = value.astype(jnp.bfloat16)
        d_out[b, p, 1] = tan.astype(jnp.bfloat16)
        d_copy(b, p, 0).start()
        d_copy(b, p, 1).start()

    def near(b, p, j):
        value, tan = project(b, PARTS * (1 + j) + p)
        d_copy(b, p, j).wait_recv()
        came = d_in[b, p, j].astype(jnp.float32)
        if j == 0:
            value = value + came
        else:
            tan = tan + came
        m_out[b, p, j, 0] = value.astype(jnp.bfloat16)
        m_out[b, p, j, 1] = tan.astype(jnp.bfloat16)
        m_copy(b, p, j).start()

    def home(b, p):
        value, tan = project(b, PARTS * 3 + p)
        own[b, p, 0] = value
        own[b, p, 1] = tan

    plan = {i: [] for i in range(STEPS)}

    def at(i, action, *args):
        plan[i].append((action, args))

    at(0, weights_two, 0), at(0, weights_one, 2)
    at(2, weights_two, 1), at(2, weights_one, 3)
    at(5, weights_core, 0)
    at(5, weights_two, 2), at(5, weights_one, 4)
    at(6, weights_ready, 0), at(6, far, order(0), 0)
    at(7, far, order(1), 0)
    at(8, weights_core, 1)
    at(8, weights_two, 3), at(8, weights_one, 5)
    at(9, weights_ready, 1), at(9, far, order(0), 1)
    at(10, far, order(1), 1)
    at(11, far, order(2), 0)
    at(11, weights_core, 2)
    at(11, weights_two, 4), at(11, weights_one, 6)
    at(12, far, order(2), 1)
    at(13, weights_core, 3)
    at(13, weights_two, 5), at(13, weights_one, 7)

    fars = [(i, args) for i in plan for action, args in plan[i] if action is far]

    def step(i, carry):
        @pl.when(i == 12)
        def _():
            halo(0).wait_recv()
            halo(1).wait_recv()
            unpack(0, WINDOW)

        attend_pair(i)
        for k in range(STEPS):
            actions = [(f, a) for f, a in plan[k] if f is not far]
            if actions:
                @pl.when(i == k)
                def _():
                    for action, args in actions:
                        action(*args)

        hit = functools.reduce(jnp.logical_or, [i == k for k, _ in fars])

        @pl.when(hit)
        def _():
            b = sum(jnp.where(i == k, args[0], 0) for k, args in fars)
            p = sum(jnp.where(i == k, args[1], 0) for k, args in fars)
            far(b, p)

        return carry

    lax.fori_loop(0, STEPS, step, 0)
    weights_core(4)
    weights_two(6)
    weights_two(7)

    def last_far(p, carry):
        far(order(BLOCKS - 1), p)
        return carry

    lax.fori_loop(0, PARTS, last_far, 0)
    weights_ready(2)
    weights_ready(3)
    weights_core(5)
    weights_ready(4)
    weights_ready(5)

    def near_step(k, carry):
        near(order(k // PARTS), k % PARTS, 0)
        near(order(k // PARTS), k % PARTS, 1)
        return carry

    lax.fori_loop(0, BLOCKS * PARTS, near_step, 0)
    weights_core(6)
    weights_core(7)
    weights_ready(6)
    weights_ready(7)

    def home_step(k, carry):
        home(order(k // PARTS), k % PARTS)
        return carry

    lax.fori_loop(0, BLOCKS * PARTS, home_step, 0)

    def last_step(k, carry):
        b, p = order(k // PARTS), k % PARTS
        m_copy(b, p, 0).wait_recv()
        m_copy(b, p, 1).wait_recv()
        here = pl.ds(pl.multiple_of(b * BLOCK, BLOCK), BLOCK)
        columns = pl.ds(pl.multiple_of(p * PART, PART), PART)
        for j, ref in ((0, out_ref), (1, tan_ref)):
            ref[here, columns] = (
                own[b, p, j]
                + m_in[b, p, 0, j].astype(jnp.float32)
                + m_in[b, p, 1, j].astype(jnp.float32)
            ).astype(jnp.bfloat16)
        return carry

    lax.fori_loop(0, BLOCKS * PARTS, last_step, 0)

    def drain(k, carry):
        for j in (0, 1):
            d_copy(k // PARTS, k % PARTS, j).wait_send()
            m_copy(k // PARTS, k % PARTS, j).wait_send()
        return carry

    lax.fori_loop(0, BLOCKS * PARTS, drain, 0)
    halo(0).wait_send()
    halo(1).wait_send()
    for n in range(PIECES):
        for half in (0, 1):
            for copy in one(n, half) + two(n, half):
                copy.wait_send()
        core(n).wait_send()


def layer(lengths, q, qt, kv, kvt, w, wt):
    anywhere = pl.BlockSpec(memory_space=pltpu.HBM)
    vmem = pl.BlockSpec(memory_space=pltpu.VMEM)
    shape = jax.ShapeDtypeStruct((TOKENS, SHARE), jnp.bfloat16)
    bf16, f32 = jnp.bfloat16, jnp.float32
    dma = pltpu.SemaphoreType.DMA
    return pl.pallas_call(
        layer_kernel,
        out_shape=(shape, shape),
        in_specs=[vmem] + [anywhere] * 6,
        out_specs=(vmem, vmem),
        scratch_shapes=[
            pltpu.VMEM((TOKENS, GROUP), bf16),
            pltpu.VMEM((TOKENS, GROUP), bf16),
            pltpu.VMEM((2, 2 * (WINDOW + TOKENS), HEAD), bf16),
            pltpu.VMEM((2, 2 * WINDOW, HEAD), f32),
            pltpu.VMEM((2, WINDOW + TOKENS, 2 * HEAD), bf16),
            pltpu.VMEM((PIECES, 2, RING, RING, 2, ROWS, PART), bf16),
            pltpu.VMEM((TOKENS, 2 * GROUP), bf16),
            pltpu.VMEM((BLOCKS, PARTS, 2, BLOCK, PART), bf16),
            pltpu.VMEM((BLOCKS, PARTS, 2, BLOCK, PART), bf16),
            pltpu.VMEM((BLOCKS, PARTS, 2, 2, BLOCK, PART), bf16),
            pltpu.VMEM((BLOCKS, PARTS, 2, 2, BLOCK, PART), bf16),
            pltpu.VMEM((BLOCKS, PARTS, 2, BLOCK, PART), f32),
            dma((4 + 2 * PIECES,)),
            dma((2, 2)),
            dma((PIECES, 2, 3)),
            dma((PIECES, 2, 3)),
            dma((PIECES, 2, 3)),
            dma((PIECES, 2, 3)),
            dma((PIECES,)),
            dma((PIECES,)),
            dma((BLOCKS, PARTS, 2)),
            dma((BLOCKS, PARTS, 2)),
            dma((BLOCKS, PARTS, 2)),
            dma((BLOCKS, PARTS, 2)),
        ],
        compiler_params=pltpu.CompilerParams(
            collective_id=0, has_side_effects=True, vmem_limit_bytes=VMEM_LIMIT
        ),
        name="layer",
    )(lengths, q, qt, kv, kvt, w, wt)


def body(
    queries, query_tangent, key_value, key_value_tangents, doc_lengths, out_weight, weight_tangent
):
    hold = lambda v: pltpu.with_memory_space_constraint(v, pltpu.HBM)
    rows = 2 * TOKENS
    return layer(
        doc_lengths[None, :],
        hold(queries),
        hold(query_tangent),
        hold(key_value.reshape(rows, HEAD)),
        hold(key_value_tangents.reshape(rows, HEAD)),
        hold(out_weight),
        hold(weight_tangent),
    )


def solution(mesh):
    in_specs = (
        P("seq", "kv"),
        P("seq", "kv"),
        P("seq", None, "kv"),
        P("seq", None, "kv"),
        P(),
        P(("kv", "seq"), None),
        P(("kv", "seq"), None),
    )
    out_specs = (P("seq", "kv"), P("seq", "kv"))
    return jax.shard_map(body, mesh=mesh, in_specs=in_specs, out_specs=out_specs, check_vma=False)
```

time: 120 us -> 96.5 us (0.80)
  Pallas kernels: 112 us -> 93.1 us
  local copies, waits for them, and re-layouts: 6.38 us -> 2.61 us
  other arithmetic: 1.22 us -> 0 us
    pallas_call x1, Pallas kernels: 112 us -> 93.1 us  [layer(): pl.pallas_call(layer_kernel, out_shape=(shape, shape), in_specs=[vmem] +...]
    slice x2 -> x0, local copies, waits for them, and re-layouts: 2.91 us -> none  [the longest x1 2.18 us: body(): key_value[:, k]]
    another operation x3 -> x0, other arithmetic: 1.22 us -> none  [body(): jnp.stack([jnp.concatenate([key_value[:, k], key_value_tangents[:, k]], a...]
    unnamed x6 -> x4, local copies, waits for them, and re-layouts: 3.33 us -> 2.61 us
where the time goes in v3:
time: 96.5 us; the launch traced here: 96.4 us
  Pallas kernels  93.1 us (96%)
  local copies, waits for them, and re-layouts  2.61 us (3%)
    pallas_call x1, Pallas kernels, layer(): pl.pallas_call(layer_kernel, out_shape=(shape, shape), in_specs=[vmem] +...  93.1 us
    unnamed x4, local copies, waits for them, and re-layouts  2.61 us

profile of v3, /device:TPU:0, one launch (start us, length us, event | category | flops | bytes accessed | tf_op | source)
XLA Modules:
  0.0 96.4 jit_solution(1912844461254644634)
XLA Ops:
  0.6 0.0 copy-start
  0.6 0.7 copy-done
  1.3 93.1 %layer.1 = (bf16[1024,512]{1,0:T(8,128)(2,1)S(1)}, bf16[1024,512]{1,0:T(8,128)(2,1)S(1)}) custom-call(s32[1,256]{1,0:T(1,128)S(1)} %bitcast.3, bf16[1024,1024]{1,0:T(8,128)(2,1)} %q_hbm.1, bf16[1024,1024]{1,0:T(8,128)(2,1)} %qt_hbm.1, bf16[2048,128]{1,0:T(8,128)(2,1)} %bitcast.4, bf16[2048,128]{1,0:T(8,128)(2,1)} %bitcast.5, bf16[32,2048]{1,0:T(8,128)(2,1)} %w_hbm.1, ...), custom_call_target="tpu_custom_call" | custom-call | tf_op jit(solution)/shard_map/layer/pallas_call | solution.py:388
  94.4 1.0 %copy.11 = bf16[1024,512]{1,0:T(8,128)(2,1)} copy(bf16[1024,512]{1,0:T(8,128)(2,1)S(1)} %get-tuple-element.4) | data formatting | bytes 2097152
  95.4 1.0 %copy.12 = bf16[1024,512]{1,0:T(8,128)(2,1)} copy(bf16[1024,512]{1,0:T(8,128)(2,1)S(1)} %get-tuple-element.5) | data formatting | bytes 2097152
Async XLA Ops:
  0.6 0.7 copy-start

commit v4 on v3

--- a/solution.py
+++ b/solution.py
@@ -76,10 +76,10 @@
 
 
 def layer_kernel(
-    lengths_ref, q_hbm, qt_hbm, kv_hbm, kvt_hbm, w_hbm, wt_hbm, out_ref, tan_ref,
-    q_ref, qt_ref, raw, wide, ctx, w_ref, aa, d_out, d_in, m_out, m_in, own,
-    load_sem, halo_sem, one_send, one_recv, two_send, two_recv, core_send, core_recv,
-    d_send, d_recv, m_send, m_recv,
+    lengths_hbm, q_hbm, qt_hbm, kv_hbm, kvt_hbm, w_hbm, wt_hbm, out_ref, tan_ref,
+    lengths_ref, q_ref, qt_ref, raw, wide, ctx, w_ref, aa, d_out, d_in, m_out, m_in, own, final,
+    kv_sem, q_sem, w_sem, halo_sem, first_send, first_recv, one_send, one_recv, two_send, two_recv, core_send, core_recv,
+    d_send, d_recv, m_send, m_recv, out_sem,
 ):
     y = lax.axis_index("kv")
     s = lax.axis_index("seq")
@@ -99,32 +99,46 @@
         share = lax.rem(y + (2, 1, 3, 0)[n // PARTS], RING)
         columns = pl.ds(pl.multiple_of(share * SHARE + n % PARTS * PART, PART), PART)
         return [
-            pltpu.make_async_copy(w_hbm.at[:, columns], w_ref.at[n, 0, z, x, c], load_sem.at[4 + n]),
-            pltpu.make_async_copy(
-                wt_hbm.at[:, columns], w_ref.at[n, 1, z, x, c], load_sem.at[4 + PIECES + n]
-            ),
+            pltpu.make_async_copy(w_hbm.at[:, columns], w_ref.at[n, 0, z, x, c], w_sem.at[n]),
+            pltpu.make_async_copy(wt_hbm.at[:, columns], w_ref.at[n, 1, z, x, c], w_sem.at[n]),
         ]
 
+    barrier = pltpu.get_barrier_semaphore()
+    steps = sorted(
+        [(i, j) for i in range(RING) for j in range(RING) if i or j],
+        key=lambda ij: -min(ij[0], RING - ij[0]) - min(ij[1], RING - ij[1]),
+    )
+    others = [seat(z + i, x + j, c) for i, j in steps]
+    greeted = list(others)
+    greeted += [right, left, after, before, partner]
+    for device in greeted:
+        pl.semaphore_signal(barrier, inc=1, device_id=device, device_id_type=MESH)
+
+    def order(b):
+        return lax.rem(b + 1, BLOCKS)
+
     tail = pl.ds(2 * WINDOW, 2 * TOKENS)
-    loads = [
-        pltpu.make_async_copy(kv_hbm, raw.at[0, tail], load_sem.at[0]),
-        pltpu.make_async_copy(kvt_hbm, raw.at[1, tail], load_sem.at[1]),
-        pltpu.make_async_copy(q_hbm, q_ref, load_sem.at[2]),
-        pltpu.make_async_copy(qt_hbm, qt_ref, load_sem.at[3]),
+    kv_loads = [
+        pltpu.make_async_copy(kv_hbm, raw.at[0, tail], kv_sem.at[0]),
+        pltpu.make_async_copy(kvt_hbm, raw.at[1, tail], kv_sem.at[1]),
+        pltpu.make_async_copy(lengths_hbm, lengths_ref, kv_sem.at[2]),
     ]
-    for load in w_loads(0) + w_loads(1) + loads:
+
+    def q_loads(k):
+        here = pl.ds(pl.multiple_of(order(k) * BLOCK, BLOCK), BLOCK)
+        return [
+            pltpu.make_async_copy(q_hbm.at[here], q_ref.at[here], q_sem.at[k]),
+            pltpu.make_async_copy(qt_hbm.at[here], qt_ref.at[here], q_sem.at[k]),
+        ]
+
+    for load in w_loads(0) + w_loads(1) + kv_loads + q_loads(0):
         load.start()
     for n in range(2, PIECES):
         for load in w_loads(n):
             load.start()
-
-    barrier = pltpu.get_barrier_semaphore()
-    greeted = [along(a, d) for a in (0, 1) for d in (1, 2, 3)]
-    greeted += [partner, right, left, after, before]
-    for device in greeted:
-        pl.semaphore_signal(barrier, inc=1, device_id=device, device_id_type=MESH)
-    pl.semaphore_wait(barrier, len(greeted))
-
+    for k in range(1, BLOCKS):
+        for load in q_loads(k):
+            load.start()
     def remote(src, dst, send, recv, device):
         return pltpu.make_async_remote_copy(
             src_ref=src, dst_ref=dst, send_sem=send, recv_sem=recv,
@@ -134,41 +148,48 @@
     def one(n, half):
         piece = w_ref.at[n, half, z, x, c]
         return [
-            remote(piece, piece, one_send.at[n, half, d - 1], one_recv.at[n, half, d - 1],
-                   along(half, d))
-            for d in (1, 3, 2)
+            remote(piece, piece, one_send.at[0], one_recv.at[n], along(half, d))
+            for d in (2, 1, 3)
         ]
 
     def two(n, half):
         line = w_ref.at[n, 0, z, :, c] if half == 0 else w_ref.at[n, 1, :, x, c]
         return [
-            remote(line, line, two_send.at[n, half, d - 1], two_recv.at[n, half, d - 1],
-                   along(1 - half, d))
-            for d in (1, 3, 2)
+            remote(line, line, two_send.at[0], two_recv.at[n], along(1 - half, d))
+            for d in (2, 1, 3)
         ]
 
     def core(n):
         mine = w_ref.at[n, :, :, :, c]
-        return remote(mine, mine, core_send.at[n], core_recv.at[n], partner)
+        return remote(mine, mine, core_send.at[0], core_recv.at[n], partner)
+
+    def arrived(ref, sem):
+        pltpu.make_async_copy(ref, ref, sem).wait()
+
+    def weights_first():
+        arrived(w_ref.at[0, :, 0, 0, 0], w_sem.at[0])
+        mine = w_ref.at[0, :, z, x, c]
+        for device in others:
+            remote(mine, mine, first_send.at[0], first_recv.at[0], device).start()
+
+    def core_first():
+        arrived(w_ref.at[pl.ds(0, 5), 0, pl.ds(0, 3), 0], first_recv.at[0])
+        core(0).start()
 
     def weights_one(n):
-        for load in w_loads(n):
-            load.wait()
+        arrived(w_ref.at[n, :, 0, 0, 0], w_sem.at[n])
         for half in (0, 1):
             for copy in one(n, half):
                 copy.start()
 
     def weights_two(n):
+        arrived(w_ref.at[n, 0, pl.ds(0, 3), 0], one_recv.at[n])
         for half in (0, 1):
-            for copy in one(n, half):
-                copy.wait_recv()
             for copy in two(n, half):
                 copy.start()
 
     def weights_core(n):
-        for half in (0, 1):
-            for copy in two(n, half):
-                copy.wait_recv()
+        arrived(w_ref.at[n, 0, pl.ds(0, 3)], two_recv.at[n])
         core(n).start()
 
     def weights_ready(n):
@@ -177,14 +198,14 @@
     def halo(k):
         return remote(
             (kv_hbm, kvt_hbm)[k].at[pl.ds(2 * (TOKENS - WINDOW), 2 * WINDOW)],
-            raw.at[k, pl.ds(0, 2 * WINDOW)], halo_sem.at[k, 0], halo_sem.at[k, 1], after,
+            raw.at[k, pl.ds(0, 2 * WINDOW)], halo_sem.at[0], halo_sem.at[1], after,
         )
 
-    weights_one(0)
+    pl.semaphore_wait(barrier, len(greeted))
     weights_one(1)
-    halo(0).start()
-    halo(1).start()
-    starts = doc_starts(lengths_ref[...])
+    weights_first()
+    weights_one(2)
+
 
     def unpack(at, rows):
         for k in (0, 1):
@@ -194,20 +215,15 @@
                     k, pl.ds(j, rows, stride=2), :
                 ].astype(jnp.bfloat16)
 
-    loads[0].wait()
-    loads[1].wait()
+    for load in kv_loads:
+        load.wait()
+    starts = doc_starts(lengths_ref[...])
 
     def unpack_step(i, carry):
         unpack(pl.multiple_of(WINDOW + i * 128, 32), 128)
         return carry
 
     lax.fori_loop(0, TOKENS // 128, unpack_step, 0)
-    loads[2].wait()
-    loads[3].wait()
-
-    def order(b):
-        return lax.rem(b + 1, BLOCKS)
-
     def attend_pair(i):
         for k in (0, 1):
             at = pl.multiple_of(lax.rem(i * PAIR + BLOCK, TOKENS) + k * STRETCH, STRETCH)
@@ -233,11 +249,11 @@
         return value, tan
 
     def d_copy(b, p, j):
-        return remote(d_out.at[b, p, j], d_in.at[b, p, j], d_send.at[b, p, j], d_recv.at[b, p, j],
+        return remote(d_out.at[b, p, j], d_in.at[b, p, j], d_send.at[0], d_recv.at[b, p, j],
                       (right, left)[j])
 
     def m_copy(b, p, j):
-        return remote(m_out.at[b, p, j], m_in.at[b, p, j], m_send.at[b, p, j], m_recv.at[b, p, j],
+        return remote(m_out.at[b, p, j], m_in.at[b, p, j], m_send.at[0], m_recv.at[b, p, j],
                       (right, left)[j])
 
     def far(b, p):
@@ -269,40 +285,47 @@
     def at(i, action, *args):
         plan[i].append((action, args))
 
-    at(0, weights_two, 0), at(0, weights_one, 2)
-    at(2, weights_two, 1), at(2, weights_one, 3)
-    at(5, weights_core, 0)
-    at(5, weights_two, 2), at(5, weights_one, 4)
-    at(6, weights_ready, 0), at(6, far, order(0), 0)
-    at(7, far, order(1), 0)
-    at(8, weights_core, 1)
-    at(8, weights_two, 3), at(8, weights_one, 5)
-    at(9, weights_ready, 1), at(9, far, order(0), 1)
-    at(10, far, order(1), 1)
+    def halo_start():
+        halo(0).start()
+        halo(1).start()
+
+    at(1, halo_start)
+    at(3, weights_one, 3), at(3, weights_two, 1)
+    at(5, core_first), at(5, weights_ready, 0), at(5, far, order(0), 0)
+    at(6, weights_one, 4), at(6, weights_two, 2)
+    at(7, weights_core, 1), at(7, far, order(1), 0)
+    at(8, weights_ready, 1), at(8, far, order(0), 1), at(8, weights_one, 5), at(8, weights_two, 3)
+    at(9, far, order(1), 1)
+    at(10, weights_one, 6), at(10, weights_two, 4), at(10, weights_core, 2)
     at(11, far, order(2), 0)
-    at(11, weights_core, 2)
-    at(11, weights_two, 4), at(11, weights_one, 6)
-    at(12, far, order(2), 1)
+    at(12, far, order(2), 1), at(12, weights_one, 7), at(12, weights_two, 5)
     at(13, weights_core, 3)
-    at(13, weights_two, 5), at(13, weights_one, 7)
+    at(14, weights_two, 6)
 
     fars = [(i, args) for i in plan for action, args in plan[i] if action is far]
 
     def step(i, carry):
+        @pl.when(i % 4 == 0)
+        def _():
+            arrived(aa.at[pl.ds(0, BLOCK)], q_sem.at[i // 4])
+
         @pl.when(i == 12)
         def _():
-            halo(0).wait_recv()
-            halo(1).wait_recv()
+            arrived(raw.at[:, pl.ds(0, 2 * WINDOW)], halo_sem.at[1])
             unpack(0, WINDOW)
 
         attend_pair(i)
-        for k in range(STEPS):
-            actions = [(f, a) for f, a in plan[k] if f is not far]
-            if actions:
-                @pl.when(i == k)
-                def _():
-                    for action, args in actions:
-                        action(*args)
+
+        def perform(wanted):
+            for k in range(STEPS):
+                actions = [(f, a) for f, a in plan[k] if f is not far and (f in (core_first, weights_ready)) == wanted]
+                if actions:
+                    @pl.when(i == k)
+                    def _():
+                        for action, args in actions:
+                            action(*args)
+
+        perform(True)
 
         hit = functools.reduce(jnp.logical_or, [i == k for k, _ in fars])
 
@@ -312,32 +335,48 @@
             p = sum(jnp.where(i == k, args[1], 0) for k, args in fars)
             far(b, p)
 
+        perform(False)
         return carry
 
     lax.fori_loop(0, STEPS, step, 0)
-    weights_core(4)
-    weights_two(6)
-    weights_two(7)
 
     def last_far(p, carry):
         far(order(BLOCKS - 1), p)
         return carry
 
     lax.fori_loop(0, PARTS, last_far, 0)
+    weights_two(7)
+    weights_core(4)
     weights_ready(2)
     weights_ready(3)
-    weights_core(5)
-    weights_ready(4)
-    weights_ready(5)
 
     def near_step(k, carry):
-        near(order(k // PARTS), k % PARTS, 0)
-        near(order(k // PARTS), k % PARTS, 1)
+        def right_step(p, carry):
+            near(order(k), p, 0)
+            return carry
+
+        def left_step(p, carry):
+            near(order(k), p, 1)
+            return carry
+
+        lax.fori_loop(0, PARTS, right_step, 0)
+
+        @pl.when(k == 0)
+        def _():
+            weights_core(5)
+            weights_ready(4)
+            weights_ready(5)
+
+        lax.fori_loop(0, PARTS, left_step, 0)
+
+        @pl.when(k == 1)
+        def _():
+            weights_core(6)
+            weights_core(7)
+
         return carry
 
-    lax.fori_loop(0, BLOCKS * PARTS, near_step, 0)
-    weights_core(6)
-    weights_core(7)
+    lax.fori_loop(0, BLOCKS, near_step, 0)
     weights_ready(6)
     weights_ready(7)
 
@@ -346,51 +385,52 @@
         return carry
 
     lax.fori_loop(0, BLOCKS * PARTS, home_step, 0)
+
+    arrived(d_out, d_send.at[0])
+    arrived(raw.at[:, pl.ds(0, 2 * WINDOW)], halo_sem.at[0])
+    arrived(w_ref.at[pl.ds(0, 5), 0, pl.ds(0, 3), 0], first_send.at[0])
+    arrived(w_ref.at[pl.ds(1, PIECES - 1), 0, pl.ds(0, 3), 0], one_send.at[0])
+    arrived(w_ref.at[pl.ds(1, PIECES - 1), 0, pl.ds(0, 3)], two_send.at[0])
+    arrived(w_ref.at[:, :, :, :, 0], core_send.at[0])
+
+    def out_copy(b, p, j):
+        here = pl.ds(pl.multiple_of(b * BLOCK, BLOCK), BLOCK)
+        columns = pl.ds(pl.multiple_of(p * PART, PART), PART)
+        return pltpu.make_async_copy(
+            final.at[b, p, j], (out_ref, tan_ref)[j].at[here, columns], out_sem.at[0]
+        )
 
     def last_step(k, carry):
         b, p = order(k // PARTS), k % PARTS
         m_copy(b, p, 0).wait_recv()
         m_copy(b, p, 1).wait_recv()
-        here = pl.ds(pl.multiple_of(b * BLOCK, BLOCK), BLOCK)
-        columns = pl.ds(pl.multiple_of(p * PART, PART), PART)
-        for j, ref in ((0, out_ref), (1, tan_ref)):
-            ref[here, columns] = (
+        for j in (0, 1):
+            final[b, p, j] = (
                 own[b, p, j]
                 + m_in[b, p, 0, j].astype(jnp.float32)
                 + m_in[b, p, 1, j].astype(jnp.float32)
             ).astype(jnp.bfloat16)
+            out_copy(b, p, j).start()
         return carry
 
     lax.fori_loop(0, BLOCKS * PARTS, last_step, 0)
 
-    def drain(k, carry):
-        for j in (0, 1):
-            d_copy(k // PARTS, k % PARTS, j).wait_send()
-            m_copy(k // PARTS, k % PARTS, j).wait_send()
-        return carry
-
-    lax.fori_loop(0, BLOCKS * PARTS, drain, 0)
-    halo(0).wait_send()
-    halo(1).wait_send()
-    for n in range(PIECES):
-        for half in (0, 1):
-            for copy in one(n, half) + two(n, half):
-                copy.wait_send()
-        core(n).wait_send()
+    arrived(m_out, m_send.at[0])
+    arrived(final, out_sem.at[0])
 
 
 def layer(lengths, q, qt, kv, kvt, w, wt):
     anywhere = pl.BlockSpec(memory_space=pltpu.HBM)
-    vmem = pl.BlockSpec(memory_space=pltpu.VMEM)
     shape = jax.ShapeDtypeStruct((TOKENS, SHARE), jnp.bfloat16)
     bf16, f32 = jnp.bfloat16, jnp.float32
     dma = pltpu.SemaphoreType.DMA
     return pl.pallas_call(
         layer_kernel,
         out_shape=(shape, shape),
-        in_specs=[vmem] + [anywhere] * 6,
-        out_specs=(vmem, vmem),
+        in_specs=[anywhere] * 7,
+        out_specs=(pl.BlockSpec(memory_space=pl.ANY),) * 2,
         scratch_shapes=[
+            pltpu.VMEM((1, NDOCS), jnp.int32),
             pltpu.VMEM((TOKENS, GROUP), bf16),
             pltpu.VMEM((TOKENS, GROUP), bf16),
             pltpu.VMEM((2, 2 * (WINDOW + TOKENS), HEAD), bf16),
@@ -403,18 +443,24 @@
             pltpu.VMEM((BLOCKS, PARTS, 2, 2, BLOCK, PART), bf16),
             pltpu.VMEM((BLOCKS, PARTS, 2, 2, BLOCK, PART), bf16),
             pltpu.VMEM((BLOCKS, PARTS, 2, BLOCK, PART), f32),
-            dma((4 + 2 * PIECES,)),
-            dma((2, 2)),
-            dma((PIECES, 2, 3)),
-            dma((PIECES, 2, 3)),
-            dma((PIECES, 2, 3)),
-            dma((PIECES, 2, 3)),
+            pltpu.VMEM((BLOCKS, PARTS, 2, BLOCK, PART), bf16),
+            dma((3,)),
+            dma((BLOCKS,)),
             dma((PIECES,)),
+            dma((2,)),
+            dma((1,)),
+            dma((1,)),
+            dma((1,)),
             dma((PIECES,)),
+            dma((1,)),
+            dma((PIECES,)),
+            dma((1,)),
+            dma((PIECES,)),
+            dma((1,)),
             dma((BLOCKS, PARTS, 2)),
+            dma((1,)),
             dma((BLOCKS, PARTS, 2)),
-            dma((BLOCKS, PARTS, 2)),
-            dma((BLOCKS, PARTS, 2)),
+            dma((1,)),
         ],
         compiler_params=pltpu.CompilerParams(
             collective_id=0, has_side_effects=True, vmem_limit_bytes=VMEM_LIMIT
@@ -423,13 +469,38 @@
     )(lengths, q, qt, kv, kvt, w, wt)
 
 
+def flush_kernel(a_ref, b_ref, a_hbm, b_hbm, sem):
+    copies = [
+        pltpu.make_async_copy(a_ref, a_hbm, sem.at[0]),
+        pltpu.make_async_copy(b_ref, b_hbm, sem.at[1]),
+    ]
+    for copy in copies:
+        copy.start()
+    for copy in copies:
+        copy.wait()
+
+
+def flush(a, b):
+    anywhere, hbm = pl.BlockSpec(memory_space=pl.ANY), pl.BlockSpec(memory_space=pltpu.HBM)
+    shape = jax.ShapeDtypeStruct(a.shape, a.dtype)
+    return pl.pallas_call(
+        flush_kernel,
+        out_shape=(shape, shape),
+        in_specs=[anywhere, anywhere],
+        out_specs=(hbm, hbm),
+        scratch_shapes=[pltpu.SemaphoreType.DMA((2,))],
+        compiler_params=pltpu.CompilerParams(vmem_limit_bytes=4 << 20),
+        name="flush",
+    )(a, b)
+
+
 def body(
     queries, query_tangent, key_value, key_value_tangents, doc_lengths, out_weight, weight_tangent
 ):
     hold = lambda v: pltpu.with_memory_space_constraint(v, pltpu.HBM)
     rows = 2 * TOKENS
-    return layer(
-        doc_lengths[None, :],
+    out, tan = layer(
+        hold(doc_lengths[None, :]),
         hold(queries),
         hold(query_tangent),
         hold(key_value.reshape(rows, HEAD)),
@@ -437,6 +508,7 @@
         hold(out_weight),
         hold(weight_tangent),
     )
+    return flush(out, tan)
 
 
 def solution(mesh):

time: 96.5 us -> 92.8 us (0.962)
  local copies, waits for them, and re-layouts: 2.61 us -> 0 us
  Pallas kernels: 93.1 us -> 91.7 us
    unnamed x4 -> x0, local copies, waits for them, and re-layouts: 2.61 us -> none
    pallas_call x1 -> x2, Pallas kernels: 93.1 us -> 91.7 us  [the longest x1 90.3 us: layer(): pl.pallas_call(layer_kernel, out_shape=(shape, shape), in_specs=[anywhere...]
where the time goes in v4:
time: 92.8 us; the launch traced here: 92.3 us
  Pallas kernels  91.7 us (99%)
    pallas_call x1, Pallas kernels, layer(): pl.pallas_call(layer_kernel, out_shape=(shape, shape), in_specs=[anywhere...  90.3 us

profile of v4, /device:TPU:0, one launch (start us, length us, event | category | flops | bytes accessed | tf_op | source)
XLA Modules:
  0.0 92.3 jit_solution(5379096077807400862)
XLA Ops:
  0.6 90.3 %layer.1 = (bf16[1024,512]{1,0:T(8,128)(2,1)S(1)}, bf16[1024,512]{1,0:T(8,128)(2,1)S(1)}) custom-call(s32[1,256]{1,0:T(1,128)} %bitcast.5, bf16[1024,1024]{1,0:T(8,128)(2,1)} %q_hbm.1, bf16[1024,1024]{1,0:T(8,128)(2,1)} %qt_hbm.1, bf16[2048,128]{1,0:T(8,128)(2,1)} %bitcast.3, bf16[2048,128]{1,0:T(8,128)(2,1)} %bitcast.4, bf16[32,2048]{1,0:T(8,128)(2,1)} %w_hbm.1, ...), custom_call_target="tpu_custom_call" | custom-call | tf_op jit(solution)/shard_map/layer/pallas_call | solution.py:427
  91.0 1.3 %flush.1 = (bf16[1024,512]{1,0:T(8,128)(2,1)}, bf16[1024,512]{1,0:T(8,128)(2,1)}) custom-call(bf16[1024,512]{1,0:T(8,128)(2,1)S(1)} %get-tuple-element.4.a_ref, bf16[1024,512]{1,0:T(8,128)(2,1)S(1)} %get-tuple-element.5.b_ref), custom_call_target="tpu_custom_call" | custom-call | tf_op jit(solution)/shard_map/flush/pallas_call | solution.py:486

commit v5 on v4

--- a/solution.py
+++ b/solution.py
@@ -24,8 +24,9 @@
 SHARE = 512
 BLOCK = 256
 BLOCKS = TOKENS // BLOCK
-PAIR = 2 * STRETCH
-STEPS = TOKENS // PAIR
+TOGETHER = 4
+STEP_ROWS = TOGETHER * STRETCH
+STEPS = TOKENS // STEP_ROWS
 RING = 4
 ROWS = 32
 PART = 256
@@ -163,18 +164,29 @@
         mine = w_ref.at[n, :, :, :, c]
         return remote(mine, mine, core_send.at[0], core_recv.at[n], partner)
 
+    def half_columns(h):
+        return pl.ds(h * (PART // 2), PART // 2)
+
     def arrived(ref, sem):
         pltpu.make_async_copy(ref, ref, sem).wait()
 
     def weights_first():
         arrived(w_ref.at[0, :, 0, 0, 0], w_sem.at[0])
-        mine = w_ref.at[0, :, z, x, c]
-        for device in others:
-            remote(mine, mine, first_send.at[0], first_recv.at[0], device).start()
-
-    def core_first():
-        arrived(w_ref.at[pl.ds(0, 5), 0, pl.ds(0, 3), 0], first_recv.at[0])
-        core(0).start()
+        for h in (0, 1):
+            mine = w_ref.at[0, :, z, x, c, :, half_columns(h)]
+            for device in others:
+                remote(mine, mine, first_send.at[0], first_recv.at[h], device).start()
+
+    def core_half(h):
+        mine = w_ref.at[0, :, :, :, c, :, half_columns(h)]
+        return remote(mine, mine, core_send.at[0], core_recv.at[h * PIECES], partner)
+
+    def core_first(h):
+        arrived(w_ref.at[pl.ds(0, 5), 0, pl.ds(0, 3), 0, :, :, half_columns(h)], first_recv.at[h])
+        core_half(h).start()
+
+    def first_ready(h):
+        core_half(h).wait_recv()
 
     def weights_one(n):
         arrived(w_ref.at[n, :, 0, 0, 0], w_sem.at[n])
@@ -224,9 +236,9 @@
         return carry
 
     lax.fori_loop(0, TOKENS // 128, unpack_step, 0)
-    def attend_pair(i):
-        for k in (0, 1):
-            at = pl.multiple_of(lax.rem(i * PAIR + BLOCK, TOKENS) + k * STRETCH, STRETCH)
+    def attend_step(i):
+        for k in range(TOGETHER):
+            at = pl.multiple_of(lax.rem(i * STEP_ROWS + BLOCK, TOKENS) + k * STRETCH, STRETCH)
             here = pl.ds(at, STRETCH)
             span = pl.ds(at, SPAN)
             out, tan = attend_block(
@@ -262,6 +274,23 @@
         d_out[b, p, 1] = tan.astype(jnp.bfloat16)
         d_copy(b, p, 0).start()
         d_copy(b, p, 1).start()
+
+    def far_half(b, h):
+        here = pl.ds(pl.multiple_of(b * BLOCK, BLOCK), BLOCK)
+        columns = half_columns(h)
+        w = w_ref[0, 0, :, :, :, :, columns].reshape(GROUP, PART // 2)
+        wt = w_ref[0, 1, :, :, :, :, columns].reshape(GROUP, PART // 2)
+        att = aa[here, GROUP:]
+        value = jnp.dot(att, w, preferred_element_type=jnp.float32)
+        tan = jnp.dot(aa[here, :GROUP], w, preferred_element_type=jnp.float32)
+        tan = tan + jnp.dot(att, wt, preferred_element_type=jnp.float32)
+        d_out[b, 0, 0, :, columns] = value.astype(jnp.bfloat16)
+        d_out[b, 0, 1, :, columns] = tan.astype(jnp.bfloat16)
+        for j in (0, 1):
+            remote(
+                d_out.at[b, 0, j, :, columns], d_in.at[b, 0, j, :, columns],
+                d_send.at[0], d_recv.at[b, 0, j], (right, left)[j],
+            ).start()
 
     def near(b, p, j):
         value, tan = project(b, PARTS * (1 + j) + p)
@@ -285,57 +314,44 @@
     def at(i, action, *args):
         plan[i].append((action, args))
 
+    def far_next(k):
+        far(order((0, 1, 2, 2)[k]), (1, 1, 0, 1)[k])
+
     def halo_start():
         halo(0).start()
         halo(1).start()
 
-    at(1, halo_start)
-    at(3, weights_one, 3), at(3, weights_two, 1)
-    at(5, core_first), at(5, weights_ready, 0), at(5, far, order(0), 0)
-    at(6, weights_one, 4), at(6, weights_two, 2)
-    at(7, weights_core, 1), at(7, far, order(1), 0)
-    at(8, weights_ready, 1), at(8, far, order(0), 1), at(8, weights_one, 5), at(8, weights_two, 3)
-    at(9, far, order(1), 1)
-    at(10, weights_one, 6), at(10, weights_two, 4), at(10, weights_core, 2)
-    at(11, far, order(2), 0)
-    at(12, far, order(2), 1), at(12, weights_one, 7), at(12, weights_two, 5)
-    at(13, weights_core, 3)
-    at(14, weights_two, 6)
-
-    fars = [(i, args) for i in plan for action, args in plan[i] if action is far]
+    at(1, weights_one, 3), at(1, weights_two, 1)
+    at(2, core_first, 0), at(2, halo_start), at(2, weights_one, 4)
+    at(3, core_first, 1)
+    at(3, first_ready, 0), at(3, far_half, order(0), 0), at(3, far_half, order(1), 0)
+    at(3, first_ready, 1), at(3, far_half, order(0), 1), at(3, far_half, order(1), 1)
+    at(3, weights_two, 2), at(3, weights_one, 5), at(3, weights_core, 1)
+    at(4, weights_ready, 1), at(4, far_next, 0), at(4, far_next, 1)
+    at(4, weights_two, 3), at(4, weights_one, 6), at(4, weights_two, 4)
+    at(5, far_next, 2), at(5, far_next, 3), at(5, weights_core, 2)
+    at(5, weights_one, 7), at(5, weights_two, 5)
+    at(6, weights_core, 3), at(6, weights_two, 6)
 
     def step(i, carry):
-        @pl.when(i % 4 == 0)
+        @pl.when(i % 2 == 0)
         def _():
-            arrived(aa.at[pl.ds(0, BLOCK)], q_sem.at[i // 4])
-
-        @pl.when(i == 12)
+            arrived(aa.at[pl.ds(0, BLOCK)], q_sem.at[i // 2])
+
+        @pl.when(i == 6)
         def _():
             arrived(raw.at[:, pl.ds(0, 2 * WINDOW)], halo_sem.at[1])
             unpack(0, WINDOW)
 
-        attend_pair(i)
-
-        def perform(wanted):
-            for k in range(STEPS):
-                actions = [(f, a) for f, a in plan[k] if f is not far and (f in (core_first, weights_ready)) == wanted]
-                if actions:
-                    @pl.when(i == k)
-                    def _():
-                        for action, args in actions:
-                            action(*args)
-
-        perform(True)
-
-        hit = functools.reduce(jnp.logical_or, [i == k for k, _ in fars])
-
-        @pl.when(hit)
-        def _():
-            b = sum(jnp.where(i == k, args[0], 0) for k, args in fars)
-            p = sum(jnp.where(i == k, args[1], 0) for k, args in fars)
-            far(b, p)
-
-        perform(False)
+        attend_step(i)
+
+        for k in range(STEPS):
+            if plan[k]:
+                @pl.when(i == k)
+                def _():
+                    for action, args in plan[k]:
+                        action(*args)
+
         return carry
 
     lax.fori_loop(0, STEPS, step, 0)
@@ -449,13 +465,13 @@
             dma((PIECES,)),
             dma((2,)),
             dma((1,)),
-            dma((1,)),
+            dma((2,)),
             dma((1,)),
             dma((PIECES,)),
             dma((1,)),
             dma((PIECES,)),
             dma((1,)),
-            dma((PIECES,)),
+            dma((PIECES + 1,)),
             dma((1,)),
             dma((BLOCKS, PARTS, 2)),
             dma((1,)),

time: 92.8 us -> 91.1 us (0.982)
  Pallas kernels: 91.7 us -> 90 us
    pallas_call x1, Pallas kernels: 90.3 us -> 88.7 us  [layer(): pl.pallas_call(layer_kernel, out_shape=(shape, shape), in_specs=[anywhere...]
where the time goes in v5:
time: 91.1 us; the launch traced here: 90.6 us
  Pallas kernels  90 us (99%)
    pallas_call x1, Pallas kernels, layer(): pl.pallas_call(layer_kernel, out_shape=(shape, shape), in_specs=[anywhere...  88.7 us

profile of v5, /device:TPU:0, one launch (start us, length us, event | category | flops | bytes accessed | tf_op | source)
XLA Modules:
  0.0 90.6 jit_solution(4481529097306190494)
XLA Ops:
  0.6 88.7 %layer.1 = (bf16[1024,512]{1,0:T(8,128)(2,1)S(1)}, bf16[1024,512]{1,0:T(8,128)(2,1)S(1)}) custom-call(s32[1,256]{1,0:T(1,128)} %bitcast.5, bf16[1024,1024]{1,0:T(8,128)(2,1)} %q_hbm.1, bf16[1024,1024]{1,0:T(8,128)(2,1)} %qt_hbm.1, bf16[2048,128]{1,0:T(8,128)(2,1)} %bitcast.3, bf16[2048,128]{1,0:T(8,128)(2,1)} %bitcast.4, bf16[32,2048]{1,0:T(8,128)(2,1)} %w_hbm.1, ...), custom_call_target="tpu_custom_call" | custom-call | tf_op jit(solution)/shard_map/layer/pallas_call | solution.py:443
  89.3 1.3 %flush.1 = (bf16[1024,512]{1,0:T(8,128)(2,1)}, bf16[1024,512]{1,0:T(8,128)(2,1)}) custom-call(bf16[1024,512]{1,0:T(8,128)(2,1)S(1)} %get-tuple-element.4.a_ref, bf16[1024,512]{1,0:T(8,128)(2,1)S(1)} %get-tuple-element.5.b_ref), custom_call_target="tpu_custom_call" | custom-call | tf_op jit(solution)/shard_map/flush/pallas_call | solution.py:502

commit v6 on v5

--- a/solution.py
+++ b/solution.py
@@ -78,9 +78,9 @@
 
 def layer_kernel(
     lengths_hbm, q_hbm, qt_hbm, kv_hbm, kvt_hbm, w_hbm, wt_hbm, out_ref, tan_ref,
-    lengths_ref, q_ref, qt_ref, raw, wide, ctx, w_ref, aa, d_out, d_in, m_out, m_in, own, final,
+    lengths_ref, q_ref, qt_ref, raw, wide, ctx, w_ref, aa, d_out, d_in, m_out, m_in, own,
     kv_sem, q_sem, w_sem, halo_sem, first_send, first_recv, one_send, one_recv, two_send, two_recv, core_send, core_recv,
-    d_send, d_recv, m_send, m_recv, out_sem,
+    d_send, d_recv, m_send, m_recv,
 ):
     y = lax.axis_index("kv")
     s = lax.axis_index("seq")
@@ -176,6 +176,8 @@
             mine = w_ref.at[0, :, z, x, c, :, half_columns(h)]
             for device in others:
                 remote(mine, mine, first_send.at[0], first_recv.at[h], device).start()
+            if h == 0:
+                weights_one(1)
 
     def core_half(h):
         mine = w_ref.at[0, :, :, :, c, :, half_columns(h)]
@@ -214,7 +216,6 @@
         )
 
     pl.semaphore_wait(barrier, len(greeted))
-    weights_one(1)
     weights_first()
     weights_one(2)
 
@@ -236,9 +237,10 @@
         return carry
 
     lax.fori_loop(0, TOKENS // 128, unpack_step, 0)
-    def attend_step(i):
-        for k in range(TOGETHER):
-            at = pl.multiple_of(lax.rem(i * STEP_ROWS + BLOCK, TOKENS) + k * STRETCH, STRETCH)
+    def attend_step(i, start=0, count=TOGETHER):
+        for k in range(count):
+            at = lax.rem(i * STEP_ROWS + BLOCK, TOKENS) + (start + k) * STRETCH
+            at = pl.multiple_of(at, STRETCH)
             here = pl.ds(at, STRETCH)
             span = pl.ds(at, SPAN)
             out, tan = attend_block(
@@ -265,7 +267,7 @@
                       (right, left)[j])
 
     def m_copy(b, p, j):
-        return remote(m_out.at[b, p, j], m_in.at[b, p, j], m_send.at[0], m_recv.at[b, p, j],
+        return remote(m_out.at[b, p, j], m_in.at[b, p, j], m_send.at[0], m_recv.at[b, p],
                       (right, left)[j])
 
     def far(b, p):
@@ -321,10 +323,9 @@
         halo(0).start()
         halo(1).start()
 
-    at(1, weights_one, 3), at(1, weights_two, 1)
-    at(2, core_first, 0), at(2, halo_start), at(2, weights_one, 4)
-    at(3, core_first, 1)
-    at(3, first_ready, 0), at(3, far_half, order(0), 0), at(3, far_half, order(1), 0)
+    at(2, core_first, 0), at(2, weights_one, 3), at(2, weights_two, 1)
+    at(2, halo_start), at(2, weights_one, 4)
+    at(3, core_first, 1), at(3, far_half, order(1), 0)
     at(3, first_ready, 1), at(3, far_half, order(0), 1), at(3, far_half, order(1), 1)
     at(3, weights_two, 2), at(3, weights_one, 5), at(3, weights_core, 1)
     at(4, weights_ready, 1), at(4, far_next, 0), at(4, far_next, 1)
@@ -343,7 +344,23 @@
             arrived(raw.at[:, pl.ds(0, 2 * WINDOW)], halo_sem.at[1])
             unpack(0, WINDOW)
 
-        attend_step(i)
+        @pl.when(i != 3)
+        def _():
+            attend_step(i)
+
+        @pl.when(i == 3)
+        def _():
+            def half_step(k, carry):
+                attend_step(3, 2 * k, 2)
+
+                @pl.when(k == 0)
+                def _():
+                    first_ready(0)
+                    far_half(order(0), 0)
+
+                return carry
+
+            lax.fori_loop(0, 2, half_step, 0)
 
         for k in range(STEPS):
             if plan[k]:
@@ -409,30 +426,22 @@
     arrived(w_ref.at[pl.ds(1, PIECES - 1), 0, pl.ds(0, 3)], two_send.at[0])
     arrived(w_ref.at[:, :, :, :, 0], core_send.at[0])
 
-    def out_copy(b, p, j):
+    def last_step(k, carry):
+        b, p = order(k // PARTS), k % PARTS
+        arrived(m_in.at[b, p], m_recv.at[b, p])
         here = pl.ds(pl.multiple_of(b * BLOCK, BLOCK), BLOCK)
         columns = pl.ds(pl.multiple_of(p * PART, PART), PART)
-        return pltpu.make_async_copy(
-            final.at[b, p, j], (out_ref, tan_ref)[j].at[here, columns], out_sem.at[0]
-        )
-
-    def last_step(k, carry):
-        b, p = order(k // PARTS), k % PARTS
-        m_copy(b, p, 0).wait_recv()
-        m_copy(b, p, 1).wait_recv()
-        for j in (0, 1):
-            final[b, p, j] = (
+        for j, ref in ((0, out_ref), (1, tan_ref)):
+            ref[here, columns] = (
                 own[b, p, j]
                 + m_in[b, p, 0, j].astype(jnp.float32)
                 + m_in[b, p, 1, j].astype(jnp.float32)
             ).astype(jnp.bfloat16)
-            out_copy(b, p, j).start()
         return carry
 
     lax.fori_loop(0, BLOCKS * PARTS, last_step, 0)
 
     arrived(m_out, m_send.at[0])
-    arrived(final, out_sem.at[0])
 
 
 def layer(lengths, q, qt, kv, kvt, w, wt):
@@ -444,7 +453,7 @@
         layer_kernel,
         out_shape=(shape, shape),
         in_specs=[anywhere] * 7,
-        out_specs=(pl.BlockSpec(memory_space=pl.ANY),) * 2,
+        out_specs=(pl.BlockSpec(memory_space=pltpu.VMEM),) * 2,
         scratch_shapes=[
             pltpu.VMEM((1, NDOCS), jnp.int32),
             pltpu.VMEM((TOKENS, GROUP), bf16),
@@ -459,7 +468,6 @@
             pltpu.VMEM((BLOCKS, PARTS, 2, 2, BLOCK, PART), bf16),
             pltpu.VMEM((BLOCKS, PARTS, 2, 2, BLOCK, PART), bf16),
             pltpu.VMEM((BLOCKS, PARTS, 2, BLOCK, PART), f32),
-            pltpu.VMEM((BLOCKS, PARTS, 2, BLOCK, PART), bf16),
             dma((3,)),
             dma((BLOCKS,)),
             dma((PIECES,)),
@@ -475,8 +483,7 @@
             dma((1,)),
             dma((BLOCKS, PARTS, 2)),
             dma((1,)),
-            dma((BLOCKS, PARTS, 2)),
-            dma((1,)),
+            dma((BLOCKS, PARTS)),
         ],
         compiler_params=pltpu.CompilerParams(
             collective_id=0, has_side_effects=True, vmem_limit_bytes=VMEM_LIMIT

time: 91.1 us -> 90.8 us (level)
  no operation moved by 1% of the time
where the time goes in v6:
time: 90.8 us; the launch traced here: 90.3 us
  Pallas kernels  89.7 us (99%)
    pallas_call x1, Pallas kernels, layer(): pl.pallas_call(layer_kernel, out_shape=(shape, shape), in_specs=[anywhere...  88.4 us

profile of v6, /device:TPU:0, one launch (start us, length us, event | category | flops | bytes accessed | tf_op | source)
XLA Modules:
  0.0 90.3 jit_solution(8165051561998119527)
XLA Ops:
  0.6 88.4 %layer.1 = (bf16[1024,512]{1,0:T(8,128)(2,1)S(1)}, bf16[1024,512]{1,0:T(8,128)(2,1)S(1)}) custom-call(s32[1,256]{1,0:T(1,128)} %bitcast.5, bf16[1024,1024]{1,0:T(8,128)(2,1)} %q_hbm.1, bf16[1024,1024]{1,0:T(8,128)(2,1)} %qt_hbm.1, bf16[2048,128]{1,0:T(8,128)(2,1)} %bitcast.3, bf16[2048,128]{1,0:T(8,128)(2,1)} %bitcast.4, bf16[32,2048]{1,0:T(8,128)(2,1)} %w_hbm.1, ...), custom_call_target="tpu_custom_call" | custom-call | tf_op jit(solution)/shard_map/layer/pallas_call | solution.py:452
  89.0 1.3 %flush.1 = (bf16[1024,512]{1,0:T(8,128)(2,1)}, bf16[1024,512]{1,0:T(8,128)(2,1)}) custom-call(bf16[1024,512]{1,0:T(8,128)(2,1)S(1)} %get-tuple-element.4.a_ref, bf16[1024,512]{1,0:T(8,128)(2,1)S(1)} %get-tuple-element.5.b_ref), custom_call_target="tpu_custom_call" | custom-call | tf_op jit(solution)/shard_map/flush/pallas_call | solution.py:509

commit v7 on v6

--- a/solution.py
+++ b/solution.py
@@ -100,8 +100,8 @@
         share = lax.rem(y + (2, 1, 3, 0)[n // PARTS], RING)
         columns = pl.ds(pl.multiple_of(share * SHARE + n % PARTS * PART, PART), PART)
         return [
-            pltpu.make_async_copy(w_hbm.at[:, columns], w_ref.at[n, 0, z, x, c], w_sem.at[n]),
-            pltpu.make_async_copy(wt_hbm.at[:, columns], w_ref.at[n, 1, z, x, c], w_sem.at[n]),
+            pltpu.make_async_copy(w_hbm.at[:, columns], w_ref.at[n, 0, z, x, c], w_sem.at[min(n, 1)]),
+            pltpu.make_async_copy(wt_hbm.at[:, columns], w_ref.at[n, 1, z, x, c], w_sem.at[min(n, 1)]),
         ]
 
     barrier = pltpu.get_barrier_semaphore()
@@ -191,7 +191,8 @@
         core_half(h).wait_recv()
 
     def weights_one(n):
-        arrived(w_ref.at[n, :, 0, 0, 0], w_sem.at[n])
+        if n == 1:
+            arrived(w_ref.at[pl.ds(1, PIECES - 1), :, 0, 0, 0], w_sem.at[1])
         for half in (0, 1):
             for copy in one(n, half):
                 copy.start()
@@ -263,7 +264,7 @@
         return value, tan
 
     def d_copy(b, p, j):
-        return remote(d_out.at[b, p, j], d_in.at[b, p, j], d_send.at[0], d_recv.at[b, p, j],
+        return remote(d_out.at[b, p, j], d_in.at[b, p, j], d_send.at[0], d_recv.at[b, j],
                       (right, left)[j])
 
     def m_copy(b, p, j):
@@ -291,12 +292,11 @@
         for j in (0, 1):
             remote(
                 d_out.at[b, 0, j, :, columns], d_in.at[b, 0, j, :, columns],
-                d_send.at[0], d_recv.at[b, 0, j], (right, left)[j],
+                d_send.at[0], d_recv.at[b, j], (right, left)[j],
             ).start()
 
     def near(b, p, j):
         value, tan = project(b, PARTS * (1 + j) + p)
-        d_copy(b, p, j).wait_recv()
         came = d_in[b, p, j].astype(jnp.float32)
         if j == 0:
             value = value + came
@@ -392,6 +392,7 @@
             near(order(k), p, 1)
             return carry
 
+        arrived(d_in.at[order(k), :, 0], d_recv.at[order(k), 0])
         lax.fori_loop(0, PARTS, right_step, 0)
 
         @pl.when(k == 0)
@@ -400,6 +401,7 @@
             weights_ready(4)
             weights_ready(5)
 
+        arrived(d_in.at[order(k), :, 1], d_recv.at[order(k), 1])
         lax.fori_loop(0, PARTS, left_step, 0)
 
         @pl.when(k == 1)
@@ -470,7 +472,7 @@
             pltpu.VMEM((BLOCKS, PARTS, 2, BLOCK, PART), f32),
             dma((3,)),
             dma((BLOCKS,)),
-            dma((PIECES,)),
+            dma((2,)),
             dma((2,)),
             dma((1,)),
             dma((2,)),
@@ -481,7 +483,7 @@
             dma((1,)),
             dma((PIECES + 1,)),
             dma((1,)),
-            dma((BLOCKS, PARTS, 2)),
+            dma((BLOCKS, 2)),
             dma((1,)),
             dma((BLOCKS, PARTS)),
         ],

time: 90.8 us -> 90.7 us (level)
  no operation moved by 1% of the time
where the time goes in v7:
time: 90.7 us; the launch traced here: 90.2 us
  Pallas kernels  89.6 us (99%)
    pallas_call x1, Pallas kernels, layer(): pl.pallas_call(layer_kernel, out_shape=(shape, shape), in_specs=[anywhere...  88.2 us

profile of v7, /device:TPU:0, one launch (start us, length us, event | category | flops | bytes accessed | tf_op | source)
XLA Modules:
  0.0 90.2 jit_solution(103605920513694903)
XLA Ops:
  0.6 88.2 %layer.1 = (bf16[1024,512]{1,0:T(8,128)(2,1)S(1)}, bf16[1024,512]{1,0:T(8,128)(2,1)S(1)}) custom-call(s32[1,256]{1,0:T(1,128)} %bitcast.5, bf16[1024,1024]{1,0:T(8,128)(2,1)} %q_hbm.1, bf16[1024,1024]{1,0:T(8,128)(2,1)} %qt_hbm.1, bf16[2048,128]{1,0:T(8,128)(2,1)} %bitcast.3, bf16[2048,128]{1,0:T(8,128)(2,1)} %bitcast.4, bf16[32,2048]{1,0:T(8,128)(2,1)} %w_hbm.1, ...), custom_call_target="tpu_custom_call" | custom-call | tf_op jit(solution)/shard_map/layer/pallas_call | solution.py:454
  88.9 1.3 %flush.1 = (bf16[1024,512]{1,0:T(8,128)(2,1)}, bf16[1024,512]{1,0:T(8,128)(2,1)}) custom-call(bf16[1024,512]{1,0:T(8,128)(2,1)S(1)} %get-tuple-element.4.a_ref, bf16[1024,512]{1,0:T(8,128)(2,1)S(1)} %get-tuple-element.5.b_ref), custom_call_target="tpu_custom_call" | custom-call | tf_op jit(solution)/shard_map/flush/pallas_call | solution.py:511
